TPU v7x, 32 devices: a whole 2x2x4 slice. The times are simulated.
32 devices in a mesh: ctx: 8 (over z, x), head: 4 (over y, core).
Axes of the slice: x: 2, y: 2, z: 4, core: 2. Of those that a mesh axis runs over, the one named last changes fastest.
Arguments:
- q_win: bfloat16 [2048, 8192], P('ctx', 'head'), may hold values from -64 to 64
- k_win: bfloat16 [2048, 2048], P('ctx', 'head'), may hold values from -6 to 6
- v_win: bfloat16 [2048, 2048], P('ctx', 'head'), may hold values from -5 to 5
- q_lin: bfloat16 [2048, 8192], P('ctx', 'head'), may hold values from -5 to 5
- k_lin: bfloat16 [2048, 2048], P('ctx', 'head'), may hold values from -5 to 5
- v_lin: bfloat16 [2048, 2048], P('ctx', 'head'), may hold values from -5 to 5
- level_table: float32 [64, 64, 4], P(None, 'head'), may hold values from 0.05 to 0.6
- level_index: int32 [2048], P('ctx'), may hold values from 0 to 63
- q_cross: bfloat16 [2048, 8192], P('ctx', 'head'), may hold values from -64 to 64
- k_shared: bfloat16 [2048, 2048], P('ctx', 'head'), may hold values from -6 to 6
- v_shared: bfloat16 [2048, 2048], P('ctx', 'head'), may hold values from -5 to 5
- head_gain: float32 [64], P('head'), may hold values from 0.5 to 13.5
Outputs:
- attended: bfloat16 [2048, 8192], P('ctx', 'head')
All inputs are finite; a program needn't handle non-finite values.
Results may differ from a plain program's by a relative error of at most 0.008.
Values may be sent and summed in bfloat16 or wider, within the bound.
No kernel may reach another device: no remote copies, remote signals or barrier semaphores. Data moves between devices by JAX's collectives and lax.ppermute only.
A program may use at most 192 MiB of HBM per device.

v0:
```python
import jax
import jax.numpy as jnp
from jax import lax
from jax.sharding import PartitionSpec as P

QH = 64
HEAD_SIZE = 128
W = 512


exact_precision_flag = lax.Precision.HIGHEST
far_below = -1e30


def shifted(value, axis, steps):
    count = lax.axis_size(axis)
    first, last = (max(0, -steps), min(count, count - steps))
    return lax.ppermute(value, axis, [(source, source + steps) for source in range(first, last)])


def partner(block, axis, apart):
    count = lax.axis_size(axis)
    route = []
    for low in range(count):
        high = low | 1 << apart
        if high != low and high < count:
            route += [(low, high), (high, low)]
    return lax.ppermute(block, axis, route)


def attend_piece(carried, query_matrix, key_block, value_block, query_pos, key_pos, horizon):
    running_max, running_sum, accumulated = carried
    groups = query_matrix.shape[1]
    key_row_slice = key_block.reshape(key_block.shape[0], groups, HEAD_SIZE)
    value_rows = value_block.reshape(value_block.shape[0], groups, HEAD_SIZE)
    attention_scores = jnp.einsum(
        "ufjn,efn->fjue", query_matrix, key_row_slice, preferred_element_type=jnp.float32
    ) * HEAD_SIZE ** (-0.5)
    allowed = (key_pos[None, :] <= query_pos[:, None]) & (key_pos[None, :] >= 0)
    if horizon is not None:
        allowed = allowed & (key_pos[None, :] > query_pos[:, None] - horizon)
    attention_scores = jnp.where(allowed, attention_scores, far_below)
    new_max = jnp.maximum(running_max, jnp.max(attention_scores, axis=-1))
    weights = jnp.where(allowed, jnp.exp(attention_scores - new_max[..., None]), 0.0)
    damping = jnp.exp(running_max - new_max)
    running_sum = running_sum * damping + jnp.sum(weights, axis=-1)
    update = jnp.einsum(
        "elow,weu->elou",
        weights.astype(jnp.bfloat16),
        value_rows,
        preferred_element_type=jnp.float32,
    )
    accumulated = accumulated * damping[..., None] + update
    return (new_max, running_sum, accumulated)


def empty_carry(groups, per_group, tok_rows):
    return (
        jnp.full((groups, per_group, tok_rows), far_below, jnp.float32),
        jnp.zeros((groups, per_group, tok_rows), jnp.float32),
        jnp.zeros((groups, per_group, tok_rows, HEAD_SIZE), jnp.float32),
    )


def finish(carried, tok_rows):
    running_max, running_sum, accumulated = carried
    result = accumulated / running_sum[..., None]
    return result.transpose(2, 0, 1, 3).reshape(tok_rows, -1)


def per_device(
    q_win,
    k_win,
    v_win,
    q_lin,
    k_lin,
    v_lin,
    level_table,
    level_index,
    q_cross,
    k_shared,
    v_shared,
    head_gain,
):
    tok_rows = q_win.shape[0]
    groups = k_win.shape[1] // HEAD_SIZE
    per_group = q_win.shape[1] // k_win.shape[1]
    ctx_index = lax.axis_index("ctx")
    first_row = ctx_index * tok_rows
    query_pos = first_row + jnp.arange(tok_rows, dtype=jnp.int32)
    behind = -(-W // tok_rows)
    packed = jnp.stack([k_win, v_win])
    window_parts = []
    for offset in range(behind, 0, -1):
        window_parts.append(shifted(packed, "ctx", offset))
    window_parts.append(packed)
    window_kv = jnp.concatenate(window_parts, axis=1)
    key_pos = first_row - behind * tok_rows + jnp.arange(window_kv.shape[1], dtype=jnp.int32)
    window_q = q_win.reshape(tok_rows, groups, per_group, HEAD_SIZE)
    window_out = finish(
        attend_piece(
            empty_carry(groups, per_group, tok_rows),
            window_q,
            window_kv[0],
            window_kv[1],
            query_pos,
            key_pos,
            W,
        ),
        tok_rows,
    )
    linear_query = q_lin.reshape(tok_rows, groups, per_group, HEAD_SIZE)
    linear_key = k_lin.reshape(tok_rows, groups, HEAD_SIZE)
    linear_value = v_lin.reshape(tok_rows, groups, HEAD_SIZE)
    own_state = jnp.einsum(
        "tgd,tge->gde", linear_key, linear_value, preferred_element_type=jnp.float32
    )
    level_bits = lax.axis_size("ctx").bit_length() - 1
    state_piece = lax.all_gather(
        own_state[None].astype(jnp.bfloat16), "ctx", axis=0, tiled=True
    ).astype(jnp.float32)
    members = jnp.arange(state_piece.shape[0], dtype=jnp.int32)
    level_masks = []
    for fold_level_no in range(1, level_bits + 1):
        lower_end = ctx_index >> fold_level_no << fold_level_no
        present = ctx_index >> fold_level_no - 1 & 1 == 1
        inside = (members >= lower_end) & (members < lower_end + (1 << fold_level_no - 1)) & present
        level_masks.append(inside.astype(jnp.float32))
    level_states = jnp.zeros((level_bits, groups, HEAD_SIZE, HEAD_SIZE), jnp.float32) + jnp.einsum(
        "ln,ngde->lgde", jnp.stack(level_masks), state_piece, precision=exact_precision_flag
    )
    causal = jnp.arange(tok_rows)[:, None] >= jnp.arange(tok_rows)[None, :]
    intra_block_scores = jnp.einsum(
        "ufjn,efn->fjue", linear_query, linear_key, preferred_element_type=jnp.float32
    )
    intra_block_scores = intra_block_scores * (HEAD_SIZE * tok_rows) ** (-0.5)
    intra_block_weights = jnp.where(causal, intra_block_scores, 0.0).astype(jnp.bfloat16)
    intra_out = jnp.einsum(
        "koyw,wku->ykou", intra_block_weights, linear_value, preferred_element_type=jnp.float32
    )
    table_rows = level_table.shape[0]
    level_count = level_table.shape[2]
    one_hot = (level_index[:, None] == jnp.arange(table_rows, dtype=jnp.int32)[None, :]).astype(
        jnp.float32
    )
    level_weights = jnp.dot(
        one_hot, level_table.reshape(table_rows, -1), precision=exact_precision_flag
    )
    level_weights = level_weights.reshape(tok_rows, groups, per_group, level_count)
    readout = jnp.einsum(
        "tgrd,lgde->ltgre",
        linear_query.astype(jnp.float32),
        level_states,
        precision=exact_precision_flag,
    )
    linear_out = level_weights[..., 0:1] * intra_out
    for level_no in range(1, level_bits + 1):
        term = readout[level_no - 1] * (HEAD_SIZE * tok_rows * 2 ** (level_no - 1)) ** (-0.5)
        linear_out = linear_out + level_weights[..., level_no : level_no + 1] * term
    linear_out = linear_out.reshape(tok_rows, -1)
    ctx_size = lax.axis_size("ctx")
    splits = 0
    while splits < level_bits and groups % 2 ** (splits + 1) == 0:
        splits += 1
    bundle = jnp.concatenate(
        [
            q_cross.reshape(tok_rows, groups, per_group * HEAD_SIZE),
            k_shared.reshape(tok_rows, groups, HEAD_SIZE),
            v_shared.reshape(tok_rows, groups, HEAD_SIZE),
        ],
        axis=2,
    )
    for section in range(splits):
        half_heads = bundle.shape[1] // 2
        bit_set = ctx_index >> section & 1 == 1
        lower_half = bundle[:, :half_heads]
        upper_half = bundle[:, half_heads:]
        kept_half = jnp.where(bit_set, upper_half, lower_half)
        sent_half = jnp.where(bit_set, lower_half, upper_half)
        partner_half = partner(sent_half, "ctx", section)
        bundle = jnp.where(
            bit_set,
            jnp.concatenate([partner_half, kept_half], axis=0),
            jnp.concatenate([kept_half, partner_half], axis=0),
        )
    span_rows = bundle.shape[0]
    local_groups = bundle.shape[1]
    group_q = bundle[:, :, : per_group * HEAD_SIZE].reshape(
        span_rows, local_groups, per_group, HEAD_SIZE
    )
    group_kv = jnp.stack(
        [
            bundle[:, :, per_group * HEAD_SIZE : (per_group + 1) * HEAD_SIZE].reshape(
                span_rows, -1
            ),
            bundle[:, :, (per_group + 1) * HEAD_SIZE :].reshape(span_rows, -1),
        ]
    )
    step_size = 2**splits
    super_index = ctx_index >> splits
    super_pos = super_index * span_rows + jnp.arange(span_rows, dtype=jnp.int32)

    def regroup_attend(carried, kv_block, key_start):
        positions = key_start + jnp.arange(kv_block.shape[1], dtype=jnp.int32)
        return lax.cond(
            key_start >= 0,
            lambda inner_state: attend_piece(
                inner_state, group_q, kv_block[0], kv_block[1], super_pos, positions, None
            ),
            lambda inner_state: inner_state,
            carried,
        )

    rounds = ctx_size // step_size

    def regroup_step(offset, state_in):
        buffer, carried = state_in
        carried = regroup_attend(carried, buffer, (super_index - offset) * span_rows)
        buffer = shifted(buffer, "ctx", step_size)
        return (buffer, carried)

    buffer, carried = lax.fori_loop(
        0, rounds - 1, regroup_step, (group_kv, empty_carry(local_groups, per_group, span_rows))
    )
    carried = regroup_attend(carried, buffer, (super_index - (rounds - 1)) * span_rows)
    gathered_out = finish(carried, span_rows).reshape(
        span_rows, local_groups, per_group * HEAD_SIZE
    )
    for section in range(splits - 1, -1, -1):
        half_rows = gathered_out.shape[0] // 2
        bit_set = ctx_index >> section & 1 == 1
        first_rows = gathered_out[:half_rows]
        second_rows = gathered_out[half_rows:]
        kept_rows = jnp.where(bit_set, second_rows, first_rows)
        sent_rows = jnp.where(bit_set, first_rows, second_rows)
        partner_rows = partner(sent_rows.astype(jnp.bfloat16), "ctx", section).astype(
            sent_rows.dtype
        )
        gathered_out = jnp.where(
            bit_set,
            jnp.concatenate([partner_rows, kept_rows], axis=1),
            jnp.concatenate([kept_rows, partner_rows], axis=1),
        )
    cross_out = gathered_out.reshape(tok_rows, -1)
    combined = (window_out + linear_out + cross_out).reshape(
        tok_rows, groups * per_group, HEAD_SIZE
    )
    combined = combined * head_gain[None, :, None]
    partial_sq = jnp.sum(combined * combined, axis=(1, 2))
    mean_square = lax.psum(partial_sq, "head") / (QH * HEAD_SIZE)
    scaled = combined * lax.rsqrt(mean_square + 1e-06)[:, None, None]
    return scaled.reshape(tok_rows, -1).astype(jnp.bfloat16)


def solution(mesh):
    return jax.shard_map(
        per_device,
        mesh=mesh,
        in_specs=(
            P("ctx", "head"),
            P("ctx", "head"),
            P("ctx", "head"),
            P("ctx", "head"),
            P("ctx", "head"),
            P("ctx", "head"),
            P(None, "head", None),
            P("ctx"),
            P("ctx", "head"),
            P("ctx", "head"),
            P("ctx", "head"),
            P("head"),
        ),
        out_specs=P("ctx", "head"),
        check_vma=False,
    )
```

profile of v0, /device:TPU:30, one launch (start us, length us, event | category | flops | bytes accessed | tf_op | source)
XLA Modules:
  0.0 186.6 jit_solution(9069176239597058000)
XLA Ops:
  6.5 1.1 copy.75
  7.7 1.1 copy.76
  8.8 0.8 pad_maximum_fusion.1
  9.6 1.3 collective-permute-start
  10.9 1.3 collective-permute-start.1
  12.2 1.5 copy.90
  13.7 0.1 copy.91
  13.9 0.1 copy.92
  14.2 1.3 broadcast_select_fusion.1
  15.5 2.6 %collective-permute-start.2 = (bf16[256,2,768]{0,2,1:T(8,128)(2,1)}, bf16[256,2,768]{0,2,1:T(8,128)(2,1)}, u32[]{:S(2)}, u32[]{:S(2)}) collective-permute-start(bf16[256,2,768]{0,2,1:T(8,128)(2,1)} %get-tuple-element.156), channel_id=1, source_target_pairs={{0,4},{4,0},{8,12},{12,8},{16,20},{20,16},{24,28},{28,24},{1,5},{5... | collective-permute-start | bytes 2359304 | tf_op jit(solution)/shard_map/ppermute | solution.py:28
  18.1 0.9 convolution_convert_fusion
  19.2 0.2 fusion.65
  19.6 0.3 compare_and_fusion.2
  19.9 0.8 reshape.328
  20.7 0.8 reshape.330
  21.6 0.7 reshape.326
  22.3 1.8 reshape.329
  24.2 1.5 broadcast_in_dim.93
  25.7 2.3 %fusion.46 = f32[4,4,256,128]{2,3,1,0:T(8,128)} fusion(pred[256,256]{0,1:T(8,128)(4,1)S(1)} %iota_compare_fusion, bf16[256,4,4,128]{3,2,1,0:T(4,128)(2,1)S(1)} %reshape.329, bf16[256,4,128,1]{2,1,0,3:T(4,128)(2,1)S(1)} %bitcast.265, bf16[256,4,128,1]{2,1,0,3:T(4,128)(2,1)S(1)} %bitcast.264), kind=kOutput, calls=%fused_computation.74 | convolution fusion | flops 540016640 | bytes 3735552 | tf_op jit(solution)/shard_map/koyw,wku->ykou/dot_general | solution.py:138
  28.0 1.4 maximum_maximum_fusion
  29.4 1.0 fusion.78
  30.4 17.2 %collective-permute-done.2 = bf16[256,2,768]{0,2,1:T(8,128)(2,1)} collective-permute-done((bf16[256,2,768]{0,2,1:T(8,128)(2,1)}, bf16[256,2,768]{0,2,1:T(8,128)(2,1)}, u32[]{:S(2)}, u32[]{:S(2)}) %collective-permute-start.2) | collective-permute-done | bytes 786464 | tf_op jit(solution)/shard_map/ppermute | solution.py:28
  47.6 1.8 maximum_select_fusion.2
  49.5 2.4 %collective-permute-start.3 = (bf16[512,1,768]{0,2,1:T(8,128)(2,1)S(1)}, bf16[512,1,768]{0,2,1:T(8,128)(2,1)S(1)}, u32[]{:S(2)}, u32[]{:S(2)}) collective-permute-start(bf16[512,1,768]{0,2,1:T(8,128)(2,1)S(1)} %get-tuple-element.154), channel_id=1, source_target_pairs={{0,8},{8,0},{4,12},{12,4},{16,24},{24,16},{20,28},{28,20},{1,9},{9... | collective-permute-start | bytes 2359304 | tf_op jit(solution)/shard_map/ppermute | solution.py:28
  51.9 2.4 %fusion.31 = (f32[4,4,256]{2,1,0:T(4,128)S(1)}, f32[4,768,256,4]{2,1,3,0:T(8,128)S(1)}) fusion(pred[256,768]{0,1:T(8,128)(4,1)S(1)} %compare_and_fusion.2, bf16[768,4,128,1]{0,2,3,1:T(8,128)(2,1)S(1)} %bitcast.253, bf16[256,4,4,128]{3,2,1,0:T(4,128)(2,1)S(1)} %reshape.326), kind=kOutput, calls=%fused_computation.48 | convolution fusion | flops 814739456 | bytes 14630912 | tf_op jit(solution)/shard_map/ufjn,efn->fjue/dot_general | solution.py:36
  54.3 22.2 %collective-permute-done.3 = bf16[512,1,768]{0,2,1:T(8,128)(2,1)S(1)} collective-permute-done((bf16[512,1,768]{0,2,1:T(8,128)(2,1)S(1)}, bf16[512,1,768]{0,2,1:T(8,128)(2,1)S(1)}, u32[]{:S(2)}, u32[]{:S(2)}) %collective-permute-start.3) | collective-permute-done | bytes 786464 | tf_op jit(solution)/shard_map/ppermute | solution.py:28
  76.5 0.5 maximum_select_fusion.3
  77.0 0.9 pad_maximum_fusion.2
  77.9 1.5 collective-permute-start.4
  79.4 3.1 %fusion.32 = f32[4,4,256]{2,1,0:T(4,128)S(1)} fusion(f32[4,768,256,4]{2,1,3,0:T(8,128)S(1)} %get-tuple-element.167, f32[4,4,256]{2,1,0:T(4,128)S(1)} %get-tuple-element.165, pred[256,768]{0,1:T(8,128)(4,1)S(1)} %compare_and_fusion.2), kind=kLoop, calls=%fused_computation.49 | loop fusion | flops 15724544 | bytes 12812288 | tf_op jit(solution)/shard_map/reduce_sum | solution.py:46
  82.6 19.1 %conditional.2 = ((f32[1,4,1024]{2,1,0:T(4,128)S(1)}, f32[1,4,1024]{2,1,0:T(4,128)S(1)}, f32[1,4,1024,128]{3,2,1,0:T(8,128)})) conditional(s32[]{:T(128)} %convert_element_type.83, (f32[1,4,1024]{2,1,0:T(4,128)S(1)}, f32[1,4,1024]{2,1,0:T(4,128)S(1)}, f32[1,4,1024,128]{3,2,1,0:T(8,128)}) %tuple.21, (s32[1024]{0:T(1024)S(1)}, ...), branch_computations={%region_2.3_spmd, %region_3.6_spmd} | conditional | flops 2205168640 | bytes 63711292 | solution.py:205
  82.6 1.0 compare_and_fusion
  83.6 2.0 %copy.93 = bf16[2,1024,128]{2,1,0:T(8,128)(2,1)} copy(bf16[2,1024,128]{1,2,0:T(8,128)(2,1)} %get-tuple-element.126) | data formatting | bytes 1048576 | tf_op jit(solution)/shard_map
  85.7 4.3 %fusion = (f32[4,1024]{1,0:T(4,128)S(1)}, f32[1024,1024,4]{1,0,2:T(8,128)S(1)}) fusion(pred[1024,1024]{0,1:T(8,128)(4,1)S(1)} %compare_and_fusion, bf16[1024,1,4,128]{0,3,2,1:T(8,128)(2,1)S(1)} %get-tuple-element.127, bf16[2,1024,128]{2,1,0:T(8,128)(2,1)} %copy.93), kind=kOutput, calls=%fused_computation.2 | convolution fusion | flops 1086320640 | bytes 19152896 | tf_op jit(solution)/shard_map/while/body/eval_jaxpr/cond/branch_1_fun/ufjn,efn->fjue/dot_general | solution.py:36
  90.0 7.5 %bitcast_add_fusion = f32[1,4,1024,128]{3,2,1,0:T(8,128)} fusion(f32[1,4,1024,128]{3,2,1,0:T(8,128)} %get-tuple-element.78, f32[1024,1024,4]{1,0,2:T(8,128)S(1)} %get-tuple-element.147, f32[4,1024]{1,0:T(4,128)S(1)} %bitcast.266, pred[1024,1024]{0,1:T(8,128)(4,1)S(1)} %compare_and_fusion, f32[4,1024]{1,0:T(4,128)S(1)} %get-tuple-element.142, ...), kind=kOutput, calls=%fused_computation.9 | convolution fusion | flops 1095761920 | bytes 22315008 | tf_op jit(solution)/shard_map/while/body/eval_jaxpr/cond/branch_1_fun/elow,weu->elou/dot_general | solution.py:47
  97.5 4.2 %fusion.2 = f32[4,1024]{1,0:T(4,128)S(1)} fusion(f32[1024,1024,4]{1,0,2:T(8,128)S(1)} %get-tuple-element.147, f32[4,1024]{1,0:T(4,128)S(1)} %bitcast.267, pred[1024,1024]{0,1:T(8,128)(4,1)S(1)} %compare_and_fusion), kind=kLoop, calls=%fused_computation.4 | loop fusion | flops 20967424 | bytes 17858560 | tf_op jit(solution)/shard_map/while/body/eval_jaxpr/cond/branch_1_fun/reduce_sum | solution.py:46
  101.8 2.9 %convolution_bitcast_fusion.1 = f32[3,4,128,128,1]{3,0,2,1,4:T(4,128)} fusion(bf16[8,4,128,128]{3,2,1,0:T(8,128)(2,1)} %bitcast.260, pred[1,8]{1,0:T(4,128)(4,1)S(1)} %get-tuple-element.168, pred[1,8]{1,0:T(4,128)(4,1)S(1)} %get-tuple-element.169, pred[1,8]{1,0:T(4,128)(4,1)S(1)} %and_and_fusion.2), kind=kOutput, calls=%fused_computation.79 | convolution fusion | flops 3145776 | bytes 1835032 | tf_op jit(solution)/shard_map/ln,ngde->lgde/dot_general | solution.py:129
  104.7 1.0 collective-permute-done.4
  105.7 31.8 %conditional.3 = (f32[1,4,1024]{2,1,0:T(4,128)S(1)}, f32[1,4,1024,128]{2,3,1,0:T(8,128)}) conditional(s32[]{:T(128)} %convert_element_type.82, (f32[1,4,1024]{2,1,0:T(4,128)S(1)}, f32[1,4,1024,128]{3,2,1,0:T(8,128)}) %tuple.23, (s32[]{:T(128)}, s32[1024]{0:T(1024)S(1)}, s32[1024]{0:T(1024)S(1)}, bf16[2,1024,128]{1,2,0:T(8,128)(2,1)}, ...), branch_computations={%region_6.7_spmd, %region_7.10_spmd} | conditional | flops 2205173760 | bytes 134989904 | solution.py:205
  105.7 1.0 compare_and_fusion.1
  106.7 2.1 %copy.95 = bf16[2,1024,128]{2,1,0:T(8,128)(2,1)} copy(bf16[2,1024,128]{1,2,0:T(8,128)(2,1)} %get-tuple-element.134) | data formatting | bytes 1048576 | tf_op jit(solution)/shard_map
  108.8 4.3 %fusion.15 = (f32[4,1024]{1,0:T(4,128)S(1)}, f32[1024,1024,4]{1,0,2:T(8,128)S(1)}) fusion(pred[1024,1024]{0,1:T(8,128)(4,1)S(1)} %compare_and_fusion.1, bf16[1024,1,4,128]{0,3,2,1:T(8,128)(2,1)S(1)} %get-tuple-element.135, bf16[2,1024,128]{2,1,0:T(8,128)(2,1)} %copy.95), kind=kOutput, calls=%fused_computation.24 | convolution fusion | flops 1086320640 | bytes 19152896 | tf_op jit(solution)/shard_map/cond/branch_1_fun/ufjn,efn->fjue/dot_general | solution.py:36
  113.1 5.7 %copy-done.2 = f32[1024,1024,4]{1,0,2:T(8,128)} copy-done((f32[1024,1024,4]{1,0,2:T(8,128)}, f32[1024,1024,4]{1,0,2:T(8,128)S(1)}, u32[]{:S(2)}) %copy-start.2) | copy-done | bytes 16777240 | tf_op jit(solution)/shard_map/cond
  118.9 7.5 %bitcast_add_fusion.2 = f32[1,4,1024,128]{3,2,1,0:T(8,128)} fusion(f32[1,4,1024,128]{3,2,1,0:T(8,128)} %get-tuple-element.86, f32[1024,1024,4]{1,0,2:T(8,128)S(1)} %get-tuple-element.151, f32[4,1024]{1,0:T(4,128)S(1)} %get-tuple-element.149, pred[1024,1024]{0,1:T(8,128)(4,1)S(1)} %compare_and_fusion.1, f32[4,1024]{1,0:T(4,128)S(1)} %get-tuple-element.148, ...), kind=kOutput, calls=%fused_computation.31 | convolution fusion | flops 1095761920 | bytes 22315008 | tf_op jit(solution)/shard_map/cond/branch_1_fun/elow,weu->elou/dot_general | solution.py:47
  126.3 2.9 %copy.121 = f32[1,4,1024,128]{2,3,1,0:T(8,128)} copy(f32[1,4,1024,128]{3,2,1,0:T(8,128)} %bitcast_add_fusion.2) | data formatting | bytes 4194304 | tf_op jit(solution)/shard_map/cond | solution.py:205
  129.2 8.0 %fusion.17 = f32[4,1024]{1,0:T(4,128)S(1)} fusion(f32[1024,1024,4]{1,0,2:T(8,128)} %copy-done.2, f32[4,1024]{1,0:T(4,128)S(1)} %get-tuple-element.149, pred[1024,1024]{0,1:T(8,128)(4,1)S(1)} %compare_and_fusion.1), kind=kLoop, calls=%fused_computation.26 | loop fusion | flops 20967424 | bytes 17858560 | tf_op jit(solution)/shard_map/cond/branch_1_fun/reduce_sum | solution.py:46
  137.5 2.0 %divide_bitcast_fusion = f32[1024,1,4,128]{0,3,2,1:T(8,128)S(1)} fusion(f32[1,4,1024,128]{2,3,1,0:T(8,128)} %get-tuple-element.141, f32[4,1024]{1,0:T(4,128)S(1)} %bitcast.263), kind=kLoop, calls=%fused_computation.73 | loop fusion | flops 524288 | bytes 4210688 | tf_op jit(solution)/shard_map/transpose | solution.py:68
  139.6 0.8 collective-permute-start.5
  140.4 2.7 %convolution_bitcast_fusion = f32[3,256,4,4,128]{1,4,3,2,0:T(8,128)S(1)} fusion(bf16[256,4,4,128]{3,2,1,0:T(4,128)(2,1)S(1)} %reshape.329, f32[3,4,128,128,1]{3,0,2,1,4:T(4,128)S(1)} %copy-done.5), kind=kOutput, calls=%fused_computation.55 | convolution fusion | flops 2415919104 | bytes 8126464 | tf_op jit(solution)/shard_map/tgrd,lgde->ltgre/dot_general | solution.py:150
  143.1 0.2 slice_select_fusion.1
  143.3 9.5 %collective-permute-done.5 = bf16[512,1,512]{0,2,1:T(8,128)(2,1)S(1)} collective-permute-done((bf16[512,1,512]{0,2,1:T(8,128)(2,1)S(1)}, bf16[512,1,512]{0,2,1:T(8,128)(2,1)S(1)}, u32[]{:S(2)}, u32[]{:S(2)}) %collective-permute-start.5) | collective-permute-done | bytes 524320 | tf_op jit(solution)/shard_map/ppermute | solution.py:28
  153.0 0.3 maximum_select_fusion
  153.3 0.9 select_convert_fusion
  154.2 0.6 collective-permute-start.6
  154.8 0.2 copy-done.19
  155.0 4.9 %fusion.40 = f32[256,4,4,128]{0,3,2,1:T(8,128)} fusion(f32[3,256,4,4,128]{1,4,3,2,0:T(8,128)S(1)} %convolution_bitcast_fusion, f32[4,4,256,128]{2,3,1,0:T(8,128)S(1)} %copy-done.19, bf16[768,4,128,1]{0,2,3,1:T(8,128)(2,1)S(1)} %bitcast.261, f32[4,768,256,4]{2,1,3,0:T(8,128)S(1)} %bitcast.245, f32[4,4,256]{2,1,0:T(4,128)S(1)} %get-tuple-element.165, ...), kind=kOutput, calls=%fused_computation.59 | convolution fusion | flops 826277888 | bytes 24166400 | tf_op jit(solution)/shard_map/elow,weu->elou/dot_general | solution.py:47
  159.9 2.9 %copy.98 = f32[256,2048]{1,0:T(8,128)} copy(f32[256,2048]{0,1:T(8,128)} %bitcast.250) | data formatting | bytes 4194304 | tf_op jit(solution)/shard_map/add | solution.py:245
  163.0 3.8 %collective-permute-done.6 = bf16[256,2,512]{0,2,1:T(8,128)(2,1)} collective-permute-done((bf16[256,2,512]{0,2,1:T(8,128)(2,1)}, bf16[256,2,512]{0,2,1:T(8,128)(2,1)}, u32[]{:S(2)}, u32[]{:S(2)}) %collective-permute-start.6) | collective-permute-done | bytes 524320 | tf_op jit(solution)/shard_map/ppermute | solution.py:28
  166.8 1.1 convert_element_type.88
  167.9 0.2 maximum_select_fusion.1
  168.1 0.6 multiply_reduce_fusion
  168.7 5.8 %psum.7 = f32[256]{0:T(256)S(1)} all-reduce(f32[256]{0:T(256)S(1)} %multiply_reduce_fusion), channel_id=1, replica_groups=mesh['ctx'=8,'head'=4] {'head'}, use_global_device_ids=true, to_apply=%region_11.12 | all-reduce | flops 256 | bytes 2048 | tf_op jit(solution)/shard_map/psum | solution.py:250
  174.5 1.8 copy.99
  176.3 3.5 %multiply_convert_fusion = bf16[256,2048]{1,0:T(8,128)(2,1)} fusion(f32[256,2048]{1,0:T(8,128)} %copy.98, f32[256,2048]{1,0:T(8,128)} %copy.99, f32[256]{0:T(256)S(1)} %add_rsqrt_fusion, f32[2048]{0:T(1024)S(1)} %broadcast_bitcast_fusion), kind=kLoop, calls=%fused_computation.71 | loop fusion | flops 2097152 | bytes 5252096 | tf_op jit(solution)/shard_map/convert_element_type | solution.py:252
  (82 shorter events, 1.3 us)
Async XLA Ops:
  6.5 12.7 %copy-start = (f32[64,16,4]{0,2,1:T(4,128)S(1)}, f32[64,16,4]{0,2,1:T(4,128)}, u32[]{:S(2)}) copy-start(f32[64,16,4]{0,2,1:T(4,128)} %param.22) | copy-start | bytes 49156
  6.5 7.2 %copy-start.11 = (bf16[256,512]{1,0:T(8,128)(2,1)S(1)}, bf16[256,512]{1,0:T(8,128)(2,1)}, u32[]{:S(2)}) copy-start(bf16[256,512]{1,0:T(8,128)(2,1)} %param.25) | copy-start | bytes 786436
  6.5 7.3 %copy-start.12 = (bf16[256,512]{1,0:T(8,128)(2,1)S(1)}, bf16[256,512]{1,0:T(8,128)(2,1)}, u32[]{:S(2)}) copy-start(bf16[256,512]{1,0:T(8,128)(2,1)} %param.26) | copy-start | bytes 786436
  6.5 95.2 %all-gather.3.cloned.1.call-start = ((), (), s32[]{:S(2)}) async-start(), calls=%async_computation | async-start | bytes 1179648 | tf_op jit(solution)/shard_map/all_gather | solution.py:119
  9.6 18.3 %collective-permute-start = (bf16[2,256,512]{1,2,0:T(8,128)(2,1)}, bf16[2,256,512]{1,2,0:T(8,128)(2,1)}, u32[]{:S(2)}, u32[]{:S(2)}) collective-permute-start(bf16[2,256,512]{1,2,0:T(8,128)(2,1)} %pad_maximum_fusion.1), channel_id=1, source_target_pairs={{0,8},{4,12},{8,16},{12,20},{16,24},{20,28},{1,9},{5,13},{9,17},{1... | collective-permute-start | bytes 1572872 | tf_op jit(solution)/shard_map/ppermute | solution.py:18
  10.9 17.1 %collective-permute-start.1 = (bf16[2,256,512]{1,2,0:T(8,128)(2,1)}, bf16[2,256,512]{1,2,0:T(8,128)(2,1)}, u32[]{:S(2)}, u32[]{:S(2)}) collective-permute-start(bf16[2,256,512]{1,2,0:T(8,128)(2,1)} %pad_maximum_fusion.1), channel_id=1, source_target_pairs={{0,4},{4,8},{8,12},{12,16},{16,20},{20,24},{24,28},{1,5},{5,9},{9,... | collective-permute-start | bytes 1572872 | tf_op jit(solution)/shard_map/ppermute | solution.py:18
  14.0 4.1 %copy-start.13 = (bf16[256,512]{1,0:T(8,128)(2,1)S(1)}, bf16[256,512]{1,0:T(8,128)(2,1)}, u32[]{:S(2)}) copy-start(bf16[256,512]{1,0:T(8,128)(2,1)} %param.20) | copy-start | bytes 786436
  14.0 4.1 %copy-start.14 = (bf16[256,512]{1,0:T(8,128)(2,1)S(1)}, bf16[256,512]{1,0:T(8,128)(2,1)}, u32[]{:S(2)}) copy-start(bf16[256,512]{1,0:T(8,128)(2,1)} %param.21) | copy-start | bytes 786436
  14.0 5.2 %copy-start.18 = (s32[256]{0:T(256)S(1)}, s32[256]{0:T(256)}, u32[]{:S(2)}) copy-start(s32[256]{0:T(256)} %param.23) | copy-start | bytes 3076
  14.1 5.4 %copy-start.17 = (f32[16]{0:T(128)S(1)}, f32[16]{0:T(128)}, u32[]{:S(2)}) copy-start(f32[16]{0:T(128)} %param.27) | copy-start | bytes 196
  14.2 7.4 %copy-start.9 = (bf16[256,2048]{1,0:T(8,128)(2,1)S(1)}, bf16[256,2048]{1,0:T(8,128)(2,1)}, u32[]{:S(2)}) copy-start(bf16[256,2048]{1,0:T(8,128)(2,1)} %param.16) | copy-start | bytes 3145732
  15.5 32.1 %collective-permute-start.2 = (bf16[256,2,768]{0,2,1:T(8,128)(2,1)}, bf16[256,2,768]{0,2,1:T(8,128)(2,1)}, u32[]{:S(2)}, u32[]{:S(2)}) collective-permute-start(bf16[256,2,768]{0,2,1:T(8,128)(2,1)} %get-tuple-element.156), channel_id=1, source_target_pairs={{0,4},{4,0},{8,12},{12,8},{16,20},{20,16},{24,28},{28,24},{1,5},{5... | collective-permute-start | bytes 2359304 | tf_op jit(solution)/shard_map/ppermute | solution.py:28
  22.3 3.3 %copy-start.15 = (bf16[256,4,128]{2,1,0:T(4,128)(2,1)S(1)}, bf16[256,4,128]{2,1,0:T(4,128)(2,1)}, u32[]{:S(2)}) copy-start(bf16[256,4,128]{2,1,0:T(4,128)(2,1)} %reshape.328) | copy-start | bytes 786436
  22.3 3.3 %copy-start.16 = (bf16[256,4,128]{2,1,0:T(4,128)(2,1)S(1)}, bf16[256,4,128]{2,1,0:T(4,128)(2,1)}, u32[]{:S(2)}) copy-start(bf16[256,4,128]{2,1,0:T(4,128)(2,1)} %reshape.330) | copy-start | bytes 786436
  28.0 19.6 %copy-start.6 = (bf16[256,2,768]{0,2,1:T(8,128)(2,1)S(1)}, bf16[256,2,768]{0,2,1:T(8,128)(2,1)}, u32[]{:S(2)}) copy-start(bf16[256,2,768]{0,2,1:T(8,128)(2,1)} %get-tuple-element.157) | copy-start | bytes 2359300
  49.5 27.0 %collective-permute-start.3 = (bf16[512,1,768]{0,2,1:T(8,128)(2,1)S(1)}, bf16[512,1,768]{0,2,1:T(8,128)(2,1)S(1)}, u32[]{:S(2)}, u32[]{:S(2)}) collective-permute-start(bf16[512,1,768]{0,2,1:T(8,128)(2,1)S(1)} %get-tuple-element.154), channel_id=1, source_target_pairs={{0,8},{8,0},{4,12},{12,4},{16,24},{24,16},{20,28},{28,20},{1,9},{9... | collective-permute-start | bytes 2359304 | tf_op jit(solution)/shard_map/ppermute | solution.py:28
  54.3 28.2 %copy-start.3 = (f32[4,768,256,4]{2,1,3,0:T(8,128)}, f32[4,768,256,4]{2,1,3,0:T(8,128)S(1)}, u32[]{:S(2)}) copy-start(f32[4,768,256,4]{2,1,3,0:T(8,128)S(1)} %get-tuple-element.167) | copy-start | bytes 37748740
  77.9 27.8 %collective-permute-start.4 = (bf16[2,1024,128]{1,2,0:T(8,128)(2,1)}, bf16[2,1024,128]{1,2,0:T(8,128)(2,1)}, u32[]{:S(2)}, u32[]{:S(2)}) collective-permute-start(bf16[2,1024,128]{1,2,0:T(8,128)(2,1)} %pad_maximum_fusion.2), channel_id=1, source_target_pairs={{0,16},{4,20},{8,24},{12,28},{1,17},{5,21},{9,25},{13,29},{2,18},{... | collective-permute-start | bytes 1572872 | tf_op jit(solution)/shard_map/while/body/eval_jaxpr/ppermute | solution.py:18
  85.7 4.4 %copy-start.7 = (bf16[2,1024,128]{2,1,0:T(8,128)(2,1)S(1)}, bf16[2,1024,128]{2,1,0:T(8,128)(2,1)}, u32[]{:S(2)}) copy-start(bf16[2,1024,128]{2,1,0:T(8,128)(2,1)} %copy.93) | copy-start | bytes 1572868 | tf_op jit(solution)/shard_map/while/body/eval_jaxpr/cond
  108.8 10.1 %copy-start.8 = (bf16[2,1024,128]{2,1,0:T(8,128)(2,1)S(1)}, bf16[2,1024,128]{2,1,0:T(8,128)(2,1)}, u32[]{:S(2)}) copy-start(bf16[2,1024,128]{2,1,0:T(8,128)(2,1)} %copy.95) | copy-start | bytes 1572868 | tf_op jit(solution)/shard_map/cond
  113.1 5.8 %copy-start.2 = (f32[1024,1024,4]{1,0,2:T(8,128)}, f32[1024,1024,4]{1,0,2:T(8,128)S(1)}, u32[]{:S(2)}) copy-start(f32[1024,1024,4]{1,0,2:T(8,128)S(1)} %get-tuple-element.151) | copy-start | bytes 50331652 | tf_op jit(solution)/shard_map/cond
  137.5 2.9 %copy-start.5 = (f32[3,4,128,128,1]{3,0,2,1,4:T(4,128)S(1)}, f32[3,4,128,128,1]{3,0,2,1,4:T(4,128)}, u32[]{:S(2)}) copy-start(f32[3,4,128,128,1]{3,0,2,1,4:T(4,128)} %convolution_bitcast_fusion.1) | copy-start | bytes 2359300
  137.5 17.3 %slice-start = ((s8[12582912]{0:T(1024)(128)(4,1)}), s8[4194304]{0:T(1024)(128)(4,1)S(1)}, s32[]{:S(2)}) async-start(s8[12582912]{0:T(1024)(128)(4,1)} %bitcast.244), calls=%async_computation.1 | async-start | bytes 8388608
  139.6 15.2 %slice-start.1 = ((s8[12582912]{0:T(1024)(128)(4,1)}), s8[4194304]{0:T(1024)(128)(4,1)S(1)}, s32[]{:S(2)}) async-start(s8[12582912]{0:T(1024)(128)(4,1)} %bitcast.244), calls=%async_computation.2 | async-start | bytes 8388608
  139.6 13.2 %collective-permute-start.5 = (bf16[512,1,512]{0,2,1:T(8,128)(2,1)S(1)}, bf16[512,1,512]{0,2,1:T(8,128)(2,1)S(1)}, u32[]{:S(2)}, u32[]{:S(2)}) collective-permute-start(bf16[512,1,512]{0,2,1:T(8,128)(2,1)S(1)} %bitcast.262), channel_id=1, source_target_pairs={{0,8},{8,0},{4,12},{12,4},{16,24},{24,16},{20,28},{28,20},{1,9},{9... | collective-permute-start | bytes 1572872 | tf_op jit(solution)/shard_map/ppermute | solution.py:28
  143.1 11.7 %slice-start.2 = ((s8[12582912]{0:T(1024)(128)(4,1)}), s8[4194304]{0:T(1024)(128)(4,1)S(1)}, s32[]{:S(2)}) async-start(s8[12582912]{0:T(1024)(128)(4,1)} %bitcast.244), calls=%async_computation.3 | async-start | bytes 8388608
  153.0 1.8 copy-start.10
  153.0 2.0 %copy-start.19 = (f32[4,4,256,128]{2,3,1,0:T(8,128)S(1)}, f32[4,4,256,128]{2,3,1,0:T(8,128)}, u32[]{:S(2)}) copy-start(f32[4,4,256,128]{2,3,1,0:T(8,128)} %fusion.46) | copy-start | bytes 6291460
  154.2 12.6 %collective-permute-start.6 = (bf16[256,2,512]{0,2,1:T(8,128)(2,1)}, bf16[256,2,512]{0,2,1:T(8,128)(2,1)}, u32[]{:S(2)}, u32[]{:S(2)}) collective-permute-start(bf16[256,2,512]{0,2,1:T(8,128)(2,1)} %select_convert_fusion), channel_id=1, source_target_pairs={{0,4},{4,0},{8,12},{12,8},{16,20},{20,16},{24,28},{28,24},{1,5},{5... | collective-permute-start | bytes 1572872 | tf_op jit(solution)/shard_map/ppermute | solution.py:28
  162.9 5.1 %copy-start.4 = (f32[256,4,4,128]{0,3,2,1:T(8,128)S(1)}, f32[256,4,4,128]{0,3,2,1:T(8,128)}, u32[]{:S(2)}) copy-start(f32[256,4,4,128]{0,3,2,1:T(8,128)} %fusion.40) | copy-start | bytes 6291460
  174.5 5.3 %copy-start.1 = (f32[64,16,4]{0,2,1:T(4,128)S(1)}, f32[64,16,4]{0,2,1:T(4,128)}, u32[]{:S(2)}) copy-start(f32[64,16,4]{0,2,1:T(4,128)} %param.22) | copy-start | bytes 49156
Sparse Core Ops, SparseCore 0:
  19.2 47.5 all-gather.2
where the time goes:
time: 188 us; the launch traced here: 187 us
  waiting for transfers between devices  53.8 us (29%)
  matrix products  39.9 us (21%)
  other arithmetic  33.8 us (18%)
  local copies, waits for them, and re-layouts  28.7 us (15%)
  between operations  14 us (7%)
  starting transfers between devices  10.5 us (6%)
  blocking collectives  5.76 us (3%)
    ppermute x4, waiting for transfers between devices, partner(): return lax.ppermute(block, axis, route)  52.7 us
    dot_general x3, matrix products, attend_piece(): jnp.einsum('elow,weu->elou', weights.astype(jnp.bfloat16), value_rows, pr...  19.8 us
    reduce_sum x3, other arithmetic, attend_piece(): running_sum = running_sum * damping + jnp.sum(weights, axis=-1)  15.3 us
    dot_general x3, matrix products, attend_piece(): jnp.einsum('ufjn,efn->fjue', query_matrix, key_row_slice, preferred_eleme...  11 us
    ppermute x4, starting transfers between devices, partner(): return lax.ppermute(block, axis, route)  6.43 us
    psum x1, blocking collectives, per_device(): mean_square = lax.psum(partial_sq, 'head') / (QH * HEAD_SIZE)  5.76 us
    cond x7, local copies, waits for them, and re-layouts  5.73 us
    unnamed x47, local copies, waits for them, and re-layouts  4.32 us
  transfers between devices with their start and end apart: 8, of which 5 were waited for; matrix products, arithmetic and copies ran while one was open for 30% of the time, Pallas kernels for 0%

commit v1 on v0

v1 whole, which is shorter than its diff:
```python
import functools
import math

import jax
import jax.numpy as jnp
from jax import lax
from jax.experimental import pallas as pl
from jax.experimental.pallas import tpu as pltpu
from jax.sharding import PartitionSpec as P

QH = 64
HEAD_SIZE = 128
W = 512
LANES = 128
far_below = -1e30
exact = lax.Precision.HIGHEST
nt_dims = (((1,), (1,)), ((), ()))


def shifted(value, axis, steps):
    count = lax.axis_size(axis)
    first, last = (max(0, -steps), min(count, count - steps))
    return lax.ppermute(value, axis, [(source, source + steps) for source in range(first, last)])


def partner(block, axis, apart):
    count = lax.axis_size(axis)
    route = []
    for low in range(count):
        high = low | 1 << apart
        if high != low and high < count:
            route += [(low, high), (high, low)]
    return lax.ppermute(block, axis, route)


def scores_of(q, k):
    return lax.dot_general(q, k, nt_dims, preferred_element_type=jnp.float32)


def with_ones(v):
    return jnp.concatenate([v, jnp.ones(v.shape, v.dtype)], axis=1)


def lower_mask(s, first, last):
    rows = s.shape[0]
    row = lax.broadcasted_iota(jnp.int32, (rows, rows), 0)
    col = lax.broadcasted_iota(jnp.int32, (rows, rows), 1)
    parts = []
    width = s.shape[1]
    if first:
        parts.append(jnp.where(col > row, s[:, :rows], far_below))
    middle = s[:, rows if first else 0 : width - rows if last else width]
    if middle.shape[1]:
        parts.append(middle)
    if last:
        parts.append(jnp.where(col <= row, s[:, width - rows :], far_below))
    return parts[0] if len(parts) == 1 else jnp.concatenate(parts, axis=1)


def softmax_part(s, v_ext, unit):
    m = jnp.max(s, axis=1, keepdims=True) * unit
    p = jnp.exp2(s * unit - m)
    pv = jnp.dot(p.astype(jnp.bfloat16), v_ext, preferred_element_type=jnp.float32)
    return m, pv


UNIT = HEAD_SIZE ** (-0.5) * math.log2(math.e)


def local_kernel(heads, tile, q_ref, kv_ref, acc_ref, st_ref):
    d = HEAD_SIZE
    rows = q_ref.shape[0]
    k = kv_ref[0]
    v_ext = with_ones(kv_ref[1])
    lane = lax.broadcasted_iota(jnp.int32, (tile, LANES), 1)
    for t in range(0, rows, tile):
        st = jnp.zeros((tile, LANES), jnp.float32)
        for h in range(heads):
            q = q_ref[t : t + tile, h * d : (h + 1) * d]
            s = lower_mask(scores_of(q, k[: t + tile]), False, True)
            m, pv = softmax_part(s, v_ext[: t + tile], UNIT)
            acc_ref[t : t + tile, h * d : (h + 1) * d] = pv[:, :d]
            st = jnp.where(lane == 2 * h, m, st)
            st = jnp.where(lane == 2 * h + 1, pv[:, d:], st)
        st_ref[0, t : t + tile] = st


def piece_body(heads, tile, q_ref, k, v_ext, acc_ref, st_ref, emit):
    d = HEAD_SIZE
    rows = q_ref.shape[0]
    for t in range(0, rows, tile):
        old = st_ref[0, t : t + tile]
        for h in range(heads):
            q = q_ref[t : t + tile, h * d : (h + 1) * d]
            s = scores_of(q, k)
            m_old = old[:, 2 * h : 2 * h + 1]
            l_old = old[:, 2 * h + 1 : 2 * h + 2]
            m = jnp.maximum(jnp.max(s, axis=1, keepdims=True) * UNIT, m_old)
            p = jnp.exp2(s * UNIT - m)
            pv = jnp.dot(p.astype(jnp.bfloat16), v_ext, preferred_element_type=jnp.float32)
            fade = jnp.exp2(m_old - m)
            acc = acc_ref[t : t + tile, h * d : (h + 1) * d] * fade + pv[:, :d]
            emit(t, h, m, l_old * fade + pv[:, d:], acc)


def piece_kernel(heads, tile, blocks, at_ref, q_ref, *refs):
    kv_refs = refs[:blocks]
    acc_ref, st_ref, acc_out, st_out = refs[blocks:]
    lane = lax.broadcasted_iota(jnp.int32, (tile, LANES), 1)
    live = at_ref[0] != 0

    @pl.when(live)
    def _():
        k = jnp.concatenate([r[0] for r in kv_refs], axis=0)
        v_ext = with_ones(jnp.concatenate([r[1] for r in kv_refs], axis=0))
        held = {}

        def emit(t, h, m, l, acc):
            acc_out[t : t + tile, h * HEAD_SIZE : (h + 1) * HEAD_SIZE] = acc
            st = held.get("st", jnp.zeros((tile, LANES), jnp.float32)) if h else jnp.zeros(
                (tile, LANES), jnp.float32
            )
            st = jnp.where(lane == 2 * h, m, st)
            held["st"] = jnp.where(lane == 2 * h + 1, l, st)
            if h == heads - 1:
                st_out[0, t : t + tile] = held["st"]

        piece_body(heads, tile, q_ref, k, v_ext, acc_ref, st_ref, emit)

    @pl.when(jnp.logical_not(live))
    def _():
        acc_out[...] = acc_ref[...]
        st_out[...] = st_ref[...]


def last_kernel(heads, tile, blocks, at_ref, q_ref, *refs):
    kv_refs = refs[:blocks]
    acc_ref, st_ref, side_ref, gain_ref, comb_ref, sq_ref = refs[blocks:]
    d = HEAD_SIZE
    live = at_ref[0] != 0
    rows = q_ref.shape[0]

    @pl.when(pl.program_id(0) == 0)
    def _():
        sq_ref[...] = jnp.zeros_like(sq_ref)

    def put(t, h, l, acc):
        cols = slice(h * d, (h + 1) * d)
        comb_ref[t : t + tile, cols] = gain_ref[0:1, cols] * (
            side_ref[t : t + tile, cols] + acc / l
        )

    @pl.when(live)
    def _():
        k = jnp.concatenate([r[0] for r in kv_refs], axis=0)
        v_ext = with_ones(jnp.concatenate([r[1] for r in kv_refs], axis=0))
        piece_body(
            heads, tile, q_ref, k, v_ext, acc_ref, st_ref, lambda t, h, m, l, acc: put(t, h, l, acc)
        )

    @pl.when(jnp.logical_not(live))
    def _():
        for t in range(0, rows, tile):
            old = st_ref[0, t : t + tile]
            for h in range(heads):
                put(
                    t,
                    h,
                    old[:, 2 * h + 1 : 2 * h + 2],
                    acc_ref[t : t + tile, h * d : (h + 1) * d],
                )

    total = jnp.zeros((rows, d), jnp.float32)
    for h in range(heads):
        c = comb_ref[:, h * d : (h + 1) * d]
        total = total + c * c
    sq_ref[...] += lax.dot_general(
        jnp.ones((8, d), jnp.float32), total, nt_dims, precision=exact
    )


def side_kernel(heads, tile, behind, levels, at_ref, qw_ref, own_ref, *refs):
    d = HEAD_SIZE
    back = refs[:behind]
    other_ref, ql_ref, kl_ref, vl_ref = refs[behind : behind + 4]
    buckets = refs[behind + 4 : behind + 4 + levels]
    idx_ref, table_ref, out_ref = refs[behind + 4 + levels :]
    rows = qw_ref.shape[0]
    here = at_ref[0]
    pick = at_ref[1] != 0

    entries = table_ref.shape[1]
    one_hot = (
        idx_ref[...] == lax.broadcasted_iota(jnp.int32, (rows, entries), 1)
    ).astype(jnp.float32)
    weights = jnp.dot(one_hot, table_ref[0], precision=exact, preferred_element_type=jnp.float32)

    kl = kl_ref[...]
    vl = vl_ref[...]
    wide = jnp.concatenate([b[0] for b in buckets], axis=1)
    row = lax.broadcasted_iota(jnp.int32, (tile, tile), 0)
    col = lax.broadcasted_iota(jnp.int32, (tile, tile), 1)
    for t in range(0, rows, tile):
        for h in range(heads):
            cols = slice(h * d, (h + 1) * d)
            q = ql_ref[t : t + tile, cols]
            a = scores_of(q, kl[: t + tile]) * (d * rows) ** (-0.5)
            tail = jnp.where(col <= row, a[:, t:], 0.0)
            a = jnp.concatenate([a[:, :t], tail], axis=1) if t else tail
            intra = jnp.dot(
                a.astype(jnp.bfloat16), vl[: t + tile], preferred_element_type=jnp.float32
            )
            first = h * (levels + 1)
            out = weights[t : t + tile, first : first + 1] * intra
            read = jnp.dot(q, wide, preferred_element_type=jnp.float32)
            for level in range(1, levels + 1):
                present = ((here >> (level - 1)) & 1).astype(jnp.float32)
                scale = (d * rows * 2 ** (level - 1)) ** (-0.5) * present
                out = out + (weights[t : t + tile, first + level : first + level + 1] * scale) * read[
                    :, (level - 1) * d : level * d
                ]
            out_ref[t : t + tile, cols] = out

    near = jnp.where(pick, back[-1][...], other_ref[...])
    pieces = [r[...] for r in back[:-1]] + [near, own_ref[...]]
    k = jnp.concatenate([p[0] for p in pieces], axis=0)
    v_ext = with_ones(jnp.concatenate([p[1] for p in pieces], axis=0))

    def window(general):
        for t in range(0, rows, tile):
            start = 0 if general else behind * rows + t - W
            stop = behind * rows + rows if general else behind * rows + t + tile
            for h in range(heads):
                cols = slice(h * d, (h + 1) * d)
                q = qw_ref[t : t + tile, cols]
                s = scores_of(q, k[start:stop])
                if general:
                    at_row = behind * rows + t + lax.broadcasted_iota(jnp.int32, s.shape, 0)
                    at_col = lax.broadcasted_iota(jnp.int32, s.shape, 1)
                    allowed = (at_col <= at_row) & (at_col > at_row - W)
                    allowed = allowed & (at_col >= (behind - here) * rows)
                    s = jnp.where(allowed, s, far_below)
                else:
                    s = lower_mask(s, True, True)
                m, pv = softmax_part(s, v_ext[start:stop], UNIT)
                out_ref[t : t + tile, cols] += pv[:, :d] / pv[:, d:]

    if (behind * rows) == W and rows % tile == 0:

        @pl.when(here >= behind)
        def _():
            window(False)

        @pl.when(here < behind)
        def _():
            window(True)

    else:
        window(True)


def norm_kernel(columns, comb_ref, sq_ref, out_ref):
    sums = jnp.transpose(sq_ref[...])[:, 0:1]
    out_ref[...] = (comb_ref[...] * lax.rsqrt(sums / columns + 1e-06)).astype(out_ref.dtype)


def per_device(
    q_win,
    k_win,
    v_win,
    q_lin,
    k_lin,
    v_lin,
    level_table,
    level_index,
    q_cross,
    k_shared,
    v_shared,
    head_gain,
):
    d = HEAD_SIZE
    rows = q_win.shape[0]
    groups = k_win.shape[1] // d
    heads = q_win.shape[1] // k_win.shape[1]
    wide = heads * d
    count = lax.axis_size("ctx")
    levels = count.bit_length() - 1
    tile = 128
    here = lax.axis_index("ctx").astype(jnp.int32)
    side_bit = here & 1
    deep = here >> 1
    behind = -(-W // rows)

    f32 = jnp.float32
    q_spec = pl.BlockSpec((rows, wide), lambda g, *_: (0, g))
    k_spec = pl.BlockSpec((rows, d), lambda g, *_: (0, g))
    kv_spec = pl.BlockSpec((2, rows, d), lambda g, *_: (0, 0, g))
    st_spec = pl.BlockSpec((1, rows, LANES), lambda g, *_: (g, 0, 0))
    acc_type = jax.ShapeDtypeStruct((rows, groups * wide), f32)
    st_type = jax.ShapeDtypeStruct((groups, rows, LANES), f32)
    params = pltpu.CompilerParams(dimension_semantics=("arbitrary",))

    def cost(keys, extra=0):
        pairs = rows * keys * groups * heads
        return pl.CostEstimate(
            flops=4 * pairs * d,
            transcendentals=pairs,
            bytes_accessed=2 * rows * groups * wide * 5 + extra,
        )

    def run_local(kv):
        return pl.pallas_call(
            functools.partial(local_kernel, heads, tile),
            grid=(groups,),
            in_specs=[q_spec, kv_spec],
            out_specs=[q_spec, st_spec],
            out_shape=[acc_type, st_type],
            compiler_params=params,
            cost_estimate=cost(rows),
            name="cross_local",
        )(q_cross, kv)

    def run_piece(live, kvs, acc, st):
        n = len(kvs)
        return pl.pallas_call(
            functools.partial(piece_kernel, heads, tile, n),
            grid_spec=pltpu.PrefetchScalarGridSpec(
                num_scalar_prefetch=1,
                grid=(groups,),
                in_specs=[q_spec] + [kv_spec] * n + [q_spec, st_spec],
                out_specs=[q_spec, st_spec],
            ),
            out_shape=[acc_type, st_type],
            compiler_params=params,
            cost_estimate=cost(n * rows),
            name="cross_piece",
        )(live.astype(jnp.int32).reshape(1), q_cross, *kvs, acc, st)

    def run_last(live, kvs, acc, st, side, gain):
        n = len(kvs)
        return pl.pallas_call(
            functools.partial(last_kernel, heads, tile, n),
            grid_spec=pltpu.PrefetchScalarGridSpec(
                num_scalar_prefetch=1,
                grid=(groups,),
                in_specs=[q_spec]
                + [kv_spec] * n
                + [q_spec, st_spec, q_spec, pl.BlockSpec((1, wide), lambda g, *_: (0, g))],
                out_specs=[q_spec, pl.BlockSpec((8, rows), lambda g, *_: (0, 0))],
            ),
            out_shape=[acc_type, jax.ShapeDtypeStruct((8, rows), f32)],
            compiler_params=params,
            cost_estimate=cost(n * rows),
            name="cross_last",
        )(live.astype(jnp.int32).reshape(1), q_cross, *kvs, acc, st, side, gain)

    def run_side(own, back, other, pick, buckets, index, table):
        one = pl.BlockSpec((1, d, d), lambda g, *_: (g, 0, 0))
        entries, per = table.shape[1:]
        return pl.pallas_call(
            functools.partial(side_kernel, heads, tile, behind, levels),
            grid_spec=pltpu.PrefetchScalarGridSpec(
                num_scalar_prefetch=1,
                grid=(groups,),
                in_specs=[q_spec, kv_spec]
                + [kv_spec] * behind
                + [kv_spec, q_spec, k_spec, k_spec]
                + [one] * levels
                + [
                    pl.BlockSpec((rows, 1), lambda g, *_: (0, 0)),
                    pl.BlockSpec((1, entries, per), lambda g, *_: (g, 0, 0)),
                ],
                out_specs=q_spec,
            ),
            out_shape=acc_type,
            compiler_params=params,
            cost_estimate=cost((behind + 2) * rows),
            name="side",
        )(
            jnp.stack([here, pick.astype(jnp.int32)]),
            q_win,
            own,
            *back,
            other,
            q_lin,
            k_lin,
            v_lin,
            *buckets,
            index,
            table,
        )

    shared = jnp.stack([k_shared, v_shared])
    near = jnp.stack([k_win, v_win])
    fixed = count == 8 and behind == 2

    state = jnp.einsum(
        "tgd,tge->gde",
        k_lin.reshape(rows, groups, d),
        v_lin.reshape(rows, groups, d),
        preferred_element_type=f32,
    )
    buckets = []
    for level in range(levels):
        arrived = partner(state.astype(jnp.bfloat16), "ctx", level)
        buckets.append(arrived)
        state = state + arrived.astype(f32)
    index = level_index.reshape(rows, 1)
    table = level_table.reshape(level_table.shape[0], groups, -1).transpose(1, 0, 2)
    gain = jnp.repeat(head_gain, d).reshape(1, -1)

    if fixed:
        sides = [(2 * i, 2 * i + 1) for i in range(count // 2)]
        z1 = shifted(shared, "ctx", 2)
        x0 = partner(shared, "ctx", 0)
        z3 = shifted(shared, "ctx", 6)
        back2 = shifted(near, "ctx", 2)
        from_side = lax.ppermute(near, "ctx", sides)
        x1 = partner(z1, "ctx", 0)
        z2 = shifted(z1, "ctx", 2)
        from_back = lax.ppermute(back2, "ctx", [(b, a) for a, b in sides])
        x3 = partner(z3, "ctx", 0)
        x2 = partner(z2, "ctx", 0)
        back, other, pick = [back2, from_side], from_back, side_bit == 1
    else:
        back = [shifted(near, "ctx", step) for step in range(behind, 0, -1)]
        other, pick = back[-1], side_bit == side_bit

    acc, st = run_local(shared)
    side = run_side(near, back, other, pick, buckets, index, table)
    if fixed:
        acc, st = run_piece(side_bit == 1, [x0], acc, st)
        acc, st = run_piece(deep >= 1, [z1, x1], acc, st)
        acc, st = run_piece(deep >= 3, [z3, x3], acc, st)
        comb, sq = run_last(deep >= 2, [z2, x2], acc, st, side, gain)
    else:
        every = lax.all_gather(shared, "ctx", axis=0, tiled=False)

        def step(source, carried):
            return tuple(run_piece(source < here, [every[source]], *carried))

        acc, st = lax.fori_loop(0, count - 2, step, (acc, st))
        comb, sq = run_last(here > count - 2, [every[count - 2]], acc, st, side, gain)

    sq = lax.psum(sq, "head")
    return pl.pallas_call(
        functools.partial(norm_kernel, QH * d),
        grid=(groups,),
        in_specs=[q_spec, pl.BlockSpec((8, rows), lambda g: (0, 0))],
        out_specs=q_spec,
        out_shape=jax.ShapeDtypeStruct((rows, groups * wide), jnp.bfloat16),
        compiler_params=params,
        name="norm",
    )(comb, sq)


def solution(mesh):
    return jax.shard_map(
        per_device,
        mesh=mesh,
        in_specs=(
            P("ctx", "head"),
            P("ctx", "head"),
            P("ctx", "head"),
            P("ctx", "head"),
            P("ctx", "head"),
            P("ctx", "head"),
            P(None, "head", None),
            P("ctx"),
            P("ctx", "head"),
            P("ctx", "head"),
            P("ctx", "head"),
            P("head"),
        ),
        out_specs=P("ctx", "head"),
        check_vma=False,
    )
```

time: 188 us -> 148 us (0.79)
  Pallas kernels: 0 us -> 71.6 us
  matrix products: 39.9 us -> 1.16 us
  other arithmetic: 33.8 us -> 3.44 us
  local copies, waits for them, and re-layouts: 28.7 us -> 5.08 us
  waiting for transfers between devices: 53.8 us -> 39.1 us
  between operations: 14 us -> 0.24 us
  starting transfers between devices: 10.5 us -> 19.9 us
    pallas_call x0 -> x7, Pallas kernels: none -> 71.6 us  [the longest x3 33 us: run_piece(): pl.pallas_call(functools.partial(piece_kernel, heads, tile, n), grid_spec...]
    dot_general x11 -> x1, matrix products: 39.9 us -> 1.16 us  [per_device(): jnp.einsum('tgd,tge->gde', k_lin.reshape(rows, groups, d), v_lin.reshape(...]
    ppermute x4 -> x7, waiting for transfers between devices: 52.7 us -> 20.1 us  [partner(): return lax.ppermute(block, axis, route)]
    ppermute x3 -> x4, waiting for transfers between devices: 0.99 us -> 19 us  [shifted(): lax.ppermute(value, axis, [(source, source + steps) for source in range(f...]
    reduce_sum x4 -> x0, other arithmetic: 15.9 us -> none  [the longest x3 15.3 us: attend_piece(): running_sum = running_sum * damping + jnp.sum(weights, axis=-1)]
    cond x8 -> x0, local copies, waits for them, and re-layouts: 8.64 us -> none
    ppermute x0 -> x2, starting transfers between devices: none -> 7.42 us  [the longest x1 6.14 us: per_device(): from_back = lax.ppermute(back2, 'ctx', [(b, a) for a, b in sides])]
    convert_element_type x5 -> x2, other arithmetic: 5.69 us -> 0.08 us  [per_device(): arrived = partner(state.astype(jnp.bfloat16), 'ctx', level)]
  transfers between devices with their start and end apart: 8 -> 13, of which waited for: 5 -> 2; matrix products, arithmetic and copies ran while one was open for 30% -> 4% of each run, Pallas kernels for 0% -> 38%
where the time goes in v1:
time: 148 us; the launch traced here: 147 us
  Pallas kernels  71.6 us (48%)
  waiting for transfers between devices  39.1 us (26%)
  starting transfers between devices  19.9 us (13%)
  blocking collectives  6.67 us (5%)
  local copies, waits for them, and re-layouts  5.08 us (3%)
  other arithmetic  3.44 us (2%)
    pallas_call x3, Pallas kernels, run_piece(): pl.pallas_call(functools.partial(piece_kernel, heads, tile, n), grid_spec...  33 us
    ppermute x7, waiting for transfers between devices, partner(): return lax.ppermute(block, axis, route)  20.1 us
    ppermute x4, waiting for transfers between devices, shifted(): lax.ppermute(value, axis, [(source, source + steps) for source in range(f...  19 us
    pallas_call x1, Pallas kernels, run_side(): pl.pallas_call(functools.partial(side_kernel, heads, tile, behind, levels...  15.3 us
    pallas_call x1, Pallas kernels, run_last(): pl.pallas_call(functools.partial(last_kernel, heads, tile, n), grid_spec=...  11.6 us
    pallas_call x1, Pallas kernels, run_local(): pl.pallas_call(functools.partial(local_kernel, heads, tile), grid=(groups...  7.69 us
    ppermute x7, starting transfers between devices, partner(): return lax.ppermute(block, axis, route)  7.32 us
    psum x1, blocking collectives, per_device(): sq = lax.psum(sq, 'head')  6.67 us
  transfers between devices with their start and end apart: 13, of which 2 were waited for; matrix products, arithmetic and copies ran while one was open for 4% of the time, Pallas kernels for 38%

profile of v1, /device:TPU:30, one launch (start us, length us, event | category | flops | bytes accessed | tf_op | source)
XLA Modules:
  0.0 147.2 jit_solution(9616043459962652809)
XLA Ops:
  0.0 0.0 copy-start.7
  0.0 0.0 copy-start.9
  0.0 0.0 copy-start.10
  0.0 1.9 %pad_maximum_fusion.kv_ref = bf16[2,256,512]{2,1,0:T(8,128)(2,1)} fusion(bf16[1,256,512]{2,1,0:T(8,128)(2,1)} %bitcast.25, bf16[1,256,512]{2,1,0:T(8,128)(2,1)} %bitcast.26), kind=kLoop, calls=%fused_computation | loop fusion | flops 262144 | bytes 1048576 | tf_op jit(solution)/shard_map/stack | solution.py:393
  1.9 1.3 collective-permute-start
  3.2 1.1 copy.19
  4.3 1.2 fusion.4
  5.5 0.6 collective-permute-start.10
  6.1 1.5 %collective-permute-start.6 = (bf16[2,256,512]{2,1,0:T(8,128)(2,1)}, bf16[2,256,512]{2,1,0:T(8,128)(2,1)S(1)}, u32[]{:S(2)}, u32[]{:S(2)}) collective-permute-start(bf16[2,256,512]{2,1,0:T(8,128)(2,1)} %pad_maximum_fusion.kv_ref), channel_id=1, source_target_pairs={{0,4},{4,0},{8,12},{12,8},{16,20},{20,16},{24,28},{28,24},{1,5},{5... | collective-permute-start | bytes 1572872 | tf_op jit(solution)/shard_map/ppermute | solution.py:33
  7.6 1.3 collective-permute-start.3
  8.9 0.0 copy-done.7
  8.9 0.0 copy-done.6
  8.9 0.9 pad_maximum_fusion.1.own_ref
  9.8 1.3 collective-permute-start.7
  11.0 19.0 %collective-permute-done.refs_0_ = bf16[2,256,512]{2,1,0:T(8,128)(2,1)S(1)} collective-permute-done((bf16[2,256,512]{2,1,0:T(8,128)(2,1)}, bf16[2,256,512]{2,1,0:T(8,128)(2,1)S(1)}, u32[]{:S(2)}, u32[]{:S(2)}) %collective-permute-start) | collective-permute-done | bytes 524320 | tf_op jit(solution)/shard_map/ppermute | solution.py:23
  30.1 0.0 copy-start
  30.1 1.3 collective-permute-start.1
  31.4 0.0 collective-permute-done.10.refs_6_
  31.4 0.0 copy-start.5
  31.4 2.7 %collective-permute-start.11 = (bf16[4,128,128]{2,1,0:T(8,128)(2,1)S(1)}, bf16[4,128,128]{2,1,0:T(8,128)(2,1)S(1)}, u32[]{:S(2)}, u32[]{:S(2)}) collective-permute-start(bf16[4,128,128]{2,1,0:T(8,128)(2,1)S(1)} %fusion.3), channel_id=1, source_target_pairs={{0,8},{8,0},{4,12},{12,4},{16,24},{24,16},{20,28},{28,20},{1,9},{9... | collective-permute-start | bytes 393224 | tf_op jit(solution)/shard_map/ppermute | solution.py:33
  34.1 20.1 %collective-permute-done.11.refs_7_ = bf16[4,128,128]{2,1,0:T(8,128)(2,1)S(1)} collective-permute-done((bf16[4,128,128]{2,1,0:T(8,128)(2,1)S(1)}, bf16[4,128,128]{2,1,0:T(8,128)(2,1)S(1)}, u32[]{:S(2)}, u32[]{:S(2)}) %collective-permute-start.11) | collective-permute-done | bytes 131104 | tf_op jit(solution)/shard_map/ppermute | solution.py:33
  54.2 0.0 copy-start.8
  54.2 0.5 collective-permute-start.5
  54.8 0.0 copy-done.9
  54.8 0.7 copy.17
  55.5 0.0 copy-done.10
  55.5 0.8 copy.18.refs_9_
  56.3 0.0 collective-permute-done.3.refs_0_
  56.3 0.0 copy-start.1
  56.3 1.5 %collective-permute-start.4 = (bf16[2,256,512]{2,1,0:T(8,128)(2,1)S(1)}, bf16[2,256,512]{2,1,0:T(8,128)(2,1)S(1)}, u32[]{:S(2)}, u32[]{:S(2)}) collective-permute-start(bf16[2,256,512]{2,1,0:T(8,128)(2,1)S(1)} %collective-permute-done.3.refs_0_), channel_id=1, source_target_pairs={{0,4},{4,0},{8,12},{12,8},{16,20},{20,16},{24,28},{28,24},{1,5},{5... | collective-permute-start | bytes 1572872 | tf_op jit(solution)/shard_map/ppermute | solution.py:33
  57.8 0.6 pad_add_fusion.at_ref
  58.4 0.0 collective-permute-done.6.refs_0_
  58.4 0.0 copy-start.2
  58.4 1.3 collective-permute-start.8
  59.7 0.0 collective-permute-done.7.refs_0_
  59.7 6.1 %collective-permute-start.9 = (bf16[2,256,512]{2,1,0:T(8,128)(2,1)}, bf16[2,256,512]{2,1,0:T(8,128)(2,1)}, u32[]{:S(2)}, u32[]{:S(2)}) collective-permute-start(bf16[2,256,512]{2,1,0:T(8,128)(2,1)} %collective-permute-done.7.refs_0_), channel_id=1, source_target_pairs={{4,0},{12,8},{20,16},{28,24},{5,1},{13,9},{21,17},{29,25},{6,2},{1... | collective-permute-start | bytes 1572872 | tf_op jit(solution)/shard_map/ppermute | solution.py:421
  65.8 7.7 %cross_local.1 = (f32[256,2048]{1,0:T(8,128)}, f32[4,256,128]{2,1,0:T(8,128)}) custom-call(bf16[256,2048]{1,0:T(8,128)(2,1)} %q_ref.9, bf16[2,256,512]{2,1,0:T(8,128)(2,1)} %pad_maximum_fusion.kv_ref), custom_call_target="tpu_custom_call" | custom-call | flops 536870912 | bytes 5242880 | tf_op jit(solution)/shard_map/cross_local/pallas_call | solution.py:312
  73.5 0.0 collective-permute-done.1.refs_0_
  73.5 0.0 collective-permute-start.2
  73.6 0.0 copy-done.2
  73.6 10.0 %cross_piece.3 = (f32[256,2048]{1,0:T(8,128)}, f32[4,256,128]{2,1,0:T(8,128)}) custom-call(s32[1]{0:T(128)} %bitcast.5.at_ref, bf16[256,2048]{1,0:T(8,128)(2,1)} %q_ref.9, bf16[2,256,512]{2,1,0:T(8,128)(2,1)} %copy-done.2, f32[256,2048]{1,0:T(8,128)} %get-tuple-element.15.refs_1_, f32[4,256,128]{2,1,0:T(8,128)} %get-tuple-element.16.refs_2_), custom_call_target="tpu_custom_call" | custom-call | flops 536870912 | bytes 5242880 | tf_op jit(solution)/shard_map/cross_piece/pallas_call | solution.py:325
  83.7 0.0 copy-done
  83.7 0.0 copy-done.5
  83.7 0.0 copy-done.8
  83.7 0.0 copy-done.1
  83.7 0.0 collective-permute-done.5.refs_1_
  83.7 0.0 copy-start.3
  83.7 0.5 collective-permute-start.12
  84.2 0.3 copy-done.3
  84.5 11.5 %cross_piece.4 = (f32[256,2048]{1,0:T(8,128)}, f32[4,256,128]{2,1,0:T(8,128)}) custom-call(s32[1]{0:T(128)} %bitcast.4.at_ref, bf16[256,2048]{1,0:T(8,128)(2,1)} %q_ref.9, bf16[2,256,512]{2,1,0:T(8,128)(2,1)} %copy-done, bf16[2,256,512]{2,1,0:T(8,128)(2,1)} %copy-done.3, f32[256,2048]{1,0:T(8,128)} %get-tuple-element.17.refs_2_, ...), custom_call_target="tpu_custom_call" | custom-call | flops 1073741824 | bytes 5242880 | tf_op jit(solution)/shard_map/cross_piece/pallas_call | solution.py:325
  96.0 0.0 collective-permute-done.4.refs_1_
  96.0 0.8 copy-done.4
  96.8 11.4 %cross_piece.5 = (f32[256,2048]{1,0:T(8,128)}, f32[4,256,128]{2,1,0:T(8,128)}) custom-call(s32[1]{0:T(128)} %bitcast.3.at_ref, bf16[256,2048]{1,0:T(8,128)(2,1)} %q_ref.9, bf16[2,256,512]{2,1,0:T(8,128)(2,1)} %copy-done.1, bf16[2,256,512]{2,1,0:T(8,128)(2,1)} %copy-done.4, f32[256,2048]{1,0:T(8,128)} %get-tuple-element.19.refs_2_, ...), custom_call_target="tpu_custom_call" | custom-call | flops 1073741824 | bytes 5242880 | tf_op jit(solution)/shard_map/cross_piece/pallas_call | solution.py:325
  108.2 0.0 collective-permute-done.12.refs_8_
  108.2 0.0 collective-permute-done.8.refs_1_
  108.3 0.0 collective-permute-done.9.refs_2_
  108.3 0.6 copy-done.12
  108.9 15.3 %side.1.refs_4_ = f32[256,2048]{1,0:T(8,128)} custom-call(s32[2]{0:T(128)} %pad_add_fusion.at_ref, bf16[256,2048]{1,0:T(8,128)(2,1)} %qw_ref.1, bf16[2,256,512]{2,1,0:T(8,128)(2,1)} %pad_maximum_fusion.1.own_ref, bf16[2,256,512]{2,1,0:T(8,128)(2,1)} %collective-permute-done.7.refs_0_, bf16[2,256,512]{2,1,0:T(8,128)(2,1)} %collective-permute-done.8.refs_1_, ...), custom_call_target="tpu_custom_call" | custom-call | flops 2147483648 | bytes 5242880 | tf_op jit(solution)/shard_map/side/pallas_call | solution.py:360
  124.2 0.0 collective-permute-done.2.refs_1_
  124.2 0.0 copy-done.11
  124.2 0.7 broadcast_in_dim.3
  124.8 11.6 %cross_last.1 = (f32[256,2048]{1,0:T(8,128)}, f32[8,256]{1,0:T(8,128)}) custom-call(s32[1]{0:T(128)} %bitcast.at_ref, bf16[256,2048]{1,0:T(8,128)(2,1)} %q_ref.9, bf16[2,256,512]{2,1,0:T(8,128)(2,1)} %collective-permute-done.1.refs_0_, bf16[2,256,512]{2,1,0:T(8,128)(2,1)} %collective-permute-done.2.refs_1_, f32[256,2048]{1,0:T(8,128)} %get-tuple-element.21.refs_2_, ...), custom_call_target="tpu_custom_call" | custom-call | flops 1073741824 | bytes 5242880 | tf_op jit(solution)/shard_map/cross_last/pallas_call | solution.py:341
  136.5 6.7 %psum.7.sq_ref = f32[8,256]{1,0:T(8,128)} all-reduce(f32[8,256]{1,0:T(8,128)} %get-tuple-element.24), channel_id=1, replica_groups=mesh['ctx'=8,'head'=4] {'head'}, use_global_device_ids=true, to_apply=%region_0.0 | all-reduce | flops 2048 | bytes 16384 | tf_op jit(solution)/shard_map/psum | solution.py:445
  143.1 4.0 %norm.1 = bf16[256,2048]{1,0:T(8,128)(2,1)} custom-call(f32[256,2048]{1,0:T(8,128)} %get-tuple-element.23.comb_ref, f32[8,256]{1,0:T(8,128)} %psum.7.sq_ref), custom_call_target="tpu_custom_call" | custom-call | tf_op jit(solution)/shard_map/norm/pallas_call | solution.py:446
  (6 shorter events, 0.1 us)
Async XLA Ops:
  0.0 8.9 %copy-start.7 = (bf16[256,512]{1,0:T(8,128)(2,1)S(1)}, bf16[256,512]{1,0:T(8,128)(2,1)}, u32[]{:S(2)}) copy-start(bf16[256,512]{1,0:T(8,128)(2,1)} %param.13) | copy-start | bytes 786436
  0.0 8.9 %copy-start.6 = (bf16[256,512]{1,0:T(8,128)(2,1)S(1)}, bf16[256,512]{1,0:T(8,128)(2,1)}, u32[]{:S(2)}) copy-start(bf16[256,512]{1,0:T(8,128)(2,1)} %param.14) | copy-start | bytes 786436
  0.0 54.8 %copy-start.9 = (f32[64,16,4]{0,2,1:T(4,128)S(1)}, f32[64,16,4]{0,2,1:T(4,128)}, u32[]{:S(2)}) copy-start(f32[64,16,4]{0,2,1:T(4,128)} %param.18) | copy-start | bytes 49156
  0.0 55.5 %copy-start.10 = (s32[256]{0:T(256)S(1)}, s32[256]{0:T(256)}, u32[]{:S(2)}) copy-start(s32[256]{0:T(256)} %param.19) | copy-start | bytes 3076
  1.9 28.1 %collective-permute-start = (bf16[2,256,512]{2,1,0:T(8,128)(2,1)}, bf16[2,256,512]{2,1,0:T(8,128)(2,1)S(1)}, u32[]{:S(2)}, u32[]{:S(2)}) collective-permute-start(bf16[2,256,512]{2,1,0:T(8,128)(2,1)} %pad_maximum_fusion.kv_ref), channel_id=1, source_target_pairs={{0,8},{4,12},{8,16},{12,20},{16,24},{20,28},{1,9},{5,13},{9,17},{1... | collective-permute-start | bytes 1572872 | tf_op jit(solution)/shard_map/ppermute | solution.py:23
  5.5 25.9 %collective-permute-start.10 = (bf16[4,128,128]{2,1,0:T(8,128)(2,1)S(1)}, bf16[4,128,128]{2,1,0:T(8,128)(2,1)S(1)}, u32[]{:S(2)}, u32[]{:S(2)}) collective-permute-start(bf16[4,128,128]{2,1,0:T(8,128)(2,1)S(1)} %get-tuple-element.25), channel_id=1, source_target_pairs={{0,4},{4,0},{8,12},{12,8},{16,20},{20,16},{24,28},{28,24},{1,5},{5... | collective-permute-start | bytes 393224 | tf_op jit(solution)/shard_map/ppermute | solution.py:33
  6.1 52.3 %collective-permute-start.6 = (bf16[2,256,512]{2,1,0:T(8,128)(2,1)}, bf16[2,256,512]{2,1,0:T(8,128)(2,1)S(1)}, u32[]{:S(2)}, u32[]{:S(2)}) collective-permute-start(bf16[2,256,512]{2,1,0:T(8,128)(2,1)} %pad_maximum_fusion.kv_ref), channel_id=1, source_target_pairs={{0,4},{4,0},{8,12},{12,8},{16,20},{20,16},{24,28},{28,24},{1,5},{5... | collective-permute-start | bytes 1572872 | tf_op jit(solution)/shard_map/ppermute | solution.py:33
  7.6 48.7 %collective-permute-start.3 = (bf16[2,256,512]{2,1,0:T(8,128)(2,1)}, bf16[2,256,512]{2,1,0:T(8,128)(2,1)S(1)}, u32[]{:S(2)}, u32[]{:S(2)}) collective-permute-start(bf16[2,256,512]{2,1,0:T(8,128)(2,1)} %pad_maximum_fusion.kv_ref), channel_id=1, source_target_pairs={{0,24},{4,28},{1,25},{5,29},{2,26},{6,30},{3,27},{7,31}} | collective-permute-start | bytes 1572872 | tf_op jit(solution)/shard_map/ppermute | solution.py:23
  9.8 49.9 %collective-permute-start.7 = (bf16[2,256,512]{2,1,0:T(8,128)(2,1)}, bf16[2,256,512]{2,1,0:T(8,128)(2,1)}, u32[]{:S(2)}, u32[]{:S(2)}) collective-permute-start(bf16[2,256,512]{2,1,0:T(8,128)(2,1)} %pad_maximum_fusion.1.own_ref), channel_id=1, source_target_pairs={{0,8},{4,12},{8,16},{12,20},{16,24},{20,28},{1,9},{5,13},{9,17},{1... | collective-permute-start | bytes 1572872 | tf_op jit(solution)/shard_map/ppermute | solution.py:23
  30.1 53.6 %copy-start = (bf16[2,256,512]{2,1,0:T(8,128)(2,1)}, bf16[2,256,512]{2,1,0:T(8,128)(2,1)S(1)}, u32[]{:S(2)}) copy-start(bf16[2,256,512]{2,1,0:T(8,128)(2,1)S(1)} %collective-permute-done.refs_0_) | copy-start | bytes 1572868
  30.1 43.5 %collective-permute-start.1 = (bf16[2,256,512]{2,1,0:T(8,128)(2,1)S(1)}, bf16[2,256,512]{2,1,0:T(8,128)(2,1)}, u32[]{:S(2)}, u32[]{:S(2)}) collective-permute-start(bf16[2,256,512]{2,1,0:T(8,128)(2,1)S(1)} %collective-permute-done.refs_0_), channel_id=1, source_target_pairs={{0,8},{4,12},{8,16},{12,20},{16,24},{20,28},{1,9},{5,13},{9,17},{1... | collective-permute-start | bytes 1572872 | tf_op jit(solution)/shard_map/ppermute | solution.py:23
  31.4 52.3 %copy-start.5 = (bf16[4,128,128]{2,1,0:T(8,128)(2,1)}, bf16[4,128,128]{2,1,0:T(8,128)(2,1)S(1)}, u32[]{:S(2)}) copy-start(bf16[4,128,128]{2,1,0:T(8,128)(2,1)S(1)} %collective-permute-done.10.refs_6_) | copy-start | bytes 393220
  31.4 22.8 %collective-permute-start.11 = (bf16[4,128,128]{2,1,0:T(8,128)(2,1)S(1)}, bf16[4,128,128]{2,1,0:T(8,128)(2,1)S(1)}, u32[]{:S(2)}, u32[]{:S(2)}) collective-permute-start(bf16[4,128,128]{2,1,0:T(8,128)(2,1)S(1)} %fusion.3), channel_id=1, source_target_pairs={{0,8},{8,0},{4,12},{12,4},{16,24},{24,16},{20,28},{28,20},{1,9},{9... | collective-permute-start | bytes 393224 | tf_op jit(solution)/shard_map/ppermute | solution.py:33
  54.2 29.5 %copy-start.8 = (bf16[4,128,128]{2,1,0:T(8,128)(2,1)}, bf16[4,128,128]{2,1,0:T(8,128)(2,1)S(1)}, u32[]{:S(2)}) copy-start(bf16[4,128,128]{2,1,0:T(8,128)(2,1)S(1)} %collective-permute-done.11.refs_7_) | copy-start | bytes 393220
  54.2 29.5 %collective-permute-start.5 = (bf16[2,256,512]{2,1,0:T(8,128)(2,1)S(1)}, bf16[2,256,512]{2,1,0:T(8,128)(2,1)S(1)}, u32[]{:S(2)}, u32[]{:S(2)}) collective-permute-start(bf16[2,256,512]{2,1,0:T(8,128)(2,1)S(1)} %collective-permute-done.refs_0_), channel_id=1, source_target_pairs={{0,4},{4,0},{8,12},{12,8},{16,20},{20,16},{24,28},{28,24},{1,5},{5... | collective-permute-start | bytes 1572872 | tf_op jit(solution)/shard_map/ppermute | solution.py:33
  56.3 27.4 %copy-start.1 = (bf16[2,256,512]{2,1,0:T(8,128)(2,1)}, bf16[2,256,512]{2,1,0:T(8,128)(2,1)S(1)}, u32[]{:S(2)}) copy-start(bf16[2,256,512]{2,1,0:T(8,128)(2,1)S(1)} %collective-permute-done.3.refs_0_) | copy-start | bytes 1572868
  56.3 39.7 %collective-permute-start.4 = (bf16[2,256,512]{2,1,0:T(8,128)(2,1)S(1)}, bf16[2,256,512]{2,1,0:T(8,128)(2,1)S(1)}, u32[]{:S(2)}, u32[]{:S(2)}) collective-permute-start(bf16[2,256,512]{2,1,0:T(8,128)(2,1)S(1)} %collective-permute-done.3.refs_0_), channel_id=1, source_target_pairs={{0,4},{4,0},{8,12},{12,8},{16,20},{20,16},{24,28},{28,24},{1,5},{5... | collective-permute-start | bytes 1572872 | tf_op jit(solution)/shard_map/ppermute | solution.py:33
  58.4 15.2 %copy-start.2 = (bf16[2,256,512]{2,1,0:T(8,128)(2,1)}, bf16[2,256,512]{2,1,0:T(8,128)(2,1)S(1)}, u32[]{:S(2)}) copy-start(bf16[2,256,512]{2,1,0:T(8,128)(2,1)S(1)} %collective-permute-done.6.refs_0_) | copy-start | bytes 1572868
  58.4 49.9 %collective-permute-start.8 = (bf16[2,256,512]{2,1,0:T(8,128)(2,1)}, bf16[2,256,512]{2,1,0:T(8,128)(2,1)}, u32[]{:S(2)}, u32[]{:S(2)}) collective-permute-start(bf16[2,256,512]{2,1,0:T(8,128)(2,1)} %pad_maximum_fusion.1.own_ref), channel_id=1, source_target_pairs={{0,4},{8,12},{16,20},{24,28},{1,5},{9,13},{17,21},{25,29},{2,6},{1... | collective-permute-start | bytes 1572872 | tf_op jit(solution)/shard_map/ppermute | solution.py:418
  59.7 48.6 %collective-permute-start.9 = (bf16[2,256,512]{2,1,0:T(8,128)(2,1)}, bf16[2,256,512]{2,1,0:T(8,128)(2,1)}, u32[]{:S(2)}, u32[]{:S(2)}) collective-permute-start(bf16[2,256,512]{2,1,0:T(8,128)(2,1)} %collective-permute-done.7.refs_0_), channel_id=1, source_target_pairs={{4,0},{12,8},{20,16},{28,24},{5,1},{13,9},{21,17},{29,25},{6,2},{1... | collective-permute-start | bytes 1572872 | tf_op jit(solution)/shard_map/ppermute | solution.py:421
  73.5 50.6 %collective-permute-start.2 = (bf16[2,256,512]{2,1,0:T(8,128)(2,1)}, bf16[2,256,512]{2,1,0:T(8,128)(2,1)}, u32[]{:S(2)}, u32[]{:S(2)}) collective-permute-start(bf16[2,256,512]{2,1,0:T(8,128)(2,1)} %collective-permute-done.1.refs_0_), channel_id=1, source_target_pairs={{0,4},{4,0},{8,12},{12,8},{16,20},{20,16},{24,28},{28,24},{1,5},{5... | collective-permute-start | bytes 1572872 | tf_op jit(solution)/shard_map/ppermute | solution.py:33
  83.7 0.8 copy-start.3
  83.7 24.5 %collective-permute-start.12 = (bf16[4,128,128]{2,1,0:T(8,128)(2,1)S(1)}, bf16[4,128,128]{2,1,0:T(8,128)(2,1)S(1)}, u32[]{:S(2)}, u32[]{:S(2)}) collective-permute-start(bf16[4,128,128]{2,1,0:T(8,128)(2,1)S(1)} %add_convert_fusion), channel_id=1, source_target_pairs={{0,16},{16,0},{4,20},{20,4},{8,24},{24,8},{12,28},{28,12},{1,17},{... | collective-permute-start | bytes 393224 | tf_op jit(solution)/shard_map/ppermute | solution.py:33
  96.0 0.8 copy-start.4
  108.2 0.7 copy-start.12
  108.9 15.3 %copy-start.11 = (f32[16]{0:T(128)S(1)}, f32[16]{0:T(128)}, u32[]{:S(2)}) copy-start(f32[16]{0:T(128)} %param.23) | copy-start | bytes 196

commit v2 on v0

v2 whole, which is shorter than its diff:
```python
import functools
import math

import jax
import jax.numpy as jnp
from jax import lax
from jax.experimental import pallas as pl
from jax.experimental.pallas import tpu as pltpu
from jax.sharding import PartitionSpec as P


QH = 64
HEAD_SIZE = 128
W = 512
LANES = 128
far_below = -1e30
exact = lax.Precision.HIGHEST
nt_dims = (((1,), (1,)), ((), ()))


def shifted(value, axis, steps):
    count = lax.axis_size(axis)
    first, last = (max(0, -steps), min(count, count - steps))
    return lax.ppermute(value, axis, [(source, source + steps) for source in range(first, last)])


def partner(block, axis, apart):
    count = lax.axis_size(axis)
    route = []
    for low in range(count):
        high = low | 1 << apart
        if high != low and high < count:
            route += [(low, high), (high, low)]
    return lax.ppermute(block, axis, route)


def scores_of(q, k):
    return lax.dot_general(q, k, nt_dims, preferred_element_type=jnp.float32)


def with_ones(v):
    return jnp.concatenate([v, jnp.ones(v.shape, v.dtype)], axis=1)


def lower_mask(s, first, last):
    rows = s.shape[0]
    row = lax.broadcasted_iota(jnp.int32, (rows, rows), 0)
    col = lax.broadcasted_iota(jnp.int32, (rows, rows), 1)
    parts = []
    width = s.shape[1]
    if first:
        parts.append(jnp.where(col > row, s[:, :rows], far_below))
    middle = s[:, rows if first else 0 : width - rows if last else width]
    if middle.shape[1]:
        parts.append(middle)
    if last:
        parts.append(jnp.where(col <= row, s[:, width - rows :], far_below))
    return parts[0] if len(parts) == 1 else jnp.concatenate(parts, axis=1)


UNIT = HEAD_SIZE ** (-0.5) * math.log2(math.e)
VMEM = pl.BlockSpec(memory_space=pltpu.VMEM)
SMEM = pl.BlockSpec(memory_space=pltpu.SMEM)
TILE = 128


def span(g, size, at=0):
    return pl.ds(pl.multiple_of(g * size + at, LANES), HEAD_SIZE)


def each_group(groups, body):
    lax.fori_loop(0, groups, lambda g, c: (body(g), c)[1], 0)


def pair(ref, g):
    cols = span(g, HEAD_SIZE)
    return ref[0, :, cols], ref[1, :, cols]


def joined(blocks):
    k = jnp.concatenate([b[0] for b in blocks], axis=0)
    v = jnp.concatenate([b[1] for b in blocks], axis=0)
    return k, with_ones(v)


def pack_kernel(k_ref, v_ref, out_ref):
    out_ref[0] = k_ref[...]
    out_ref[1] = v_ref[...]


def state_kernel(k_ref, v_ref, wide_ref, half_ref):
    for g in range(wide_ref.shape[0]):
        cols = slice(g * HEAD_SIZE, (g + 1) * HEAD_SIZE)
        state = lax.dot_general(
            k_ref[:, cols],
            v_ref[:, cols],
            (((0,), (0,)), ((), ())),
            preferred_element_type=jnp.float32,
        )
        wide_ref[g] = state
        half_ref[g] = state.astype(half_ref.dtype)


def local_kernel(heads, groups, q_ref, kv_ref, acc_ref, m_ref, l_ref):
    d = HEAD_SIZE
    rows = q_ref.shape[0]

    def body(g):
        k, v_ext = joined([pair(kv_ref, g)])
        for h in range(heads):
            cols = span(g, heads * d, h * d)
            for t in range(0, rows, TILE):
                at = slice(t, t + TILE)
                s = lower_mask(scores_of(q_ref[at, cols], k[: t + TILE]), False, True)
                m = jnp.max(s, axis=1, keepdims=True) * UNIT
                p = jnp.exp2(s * UNIT - m)
                pv = jnp.dot(
                    p.astype(jnp.bfloat16), v_ext[: t + TILE], preferred_element_type=jnp.float32
                )
                acc_ref[at, cols] = pv[:, :d]
                l_ref[at, cols] = pv[:, d:]
                m_ref[at, cols] = jnp.broadcast_to(m, (TILE, d))

    each_group(groups, body)


def extend(q_ref, acc_ref, m_ref, l_ref, at, cols, k, v_ext):
    d = HEAD_SIZE
    s = scores_of(q_ref[at, cols], k)
    m_old = m_ref[at, cols]
    m = jnp.maximum(jnp.max(s, axis=1, keepdims=True) * UNIT, m_old)
    p = jnp.exp2(s * UNIT - jnp.concatenate([m] * (s.shape[1] // d), axis=1))
    pv = jnp.dot(p.astype(jnp.bfloat16), v_ext, preferred_element_type=jnp.float32)
    fade = jnp.exp2(m_old - m)
    return (
        acc_ref[at, cols] * fade + pv[:, :d],
        m,
        l_ref[at, cols] * fade + pv[:, d:],
    )


def piece_kernel(heads, groups, lives, at_ref, q_ref, *refs):
    kv_refs = refs[: len(lives)]
    acc_in, m_in, l_in, acc_ref, m_ref, l_ref = refs[len(lives) :]
    rows = q_ref.shape[0]
    live = [f(at_ref) for f in lives]

    def run(blocks_of):
        def body(g):
            k, v_ext = joined(blocks_of(g))
            for h in range(heads):
                cols = span(g, heads * HEAD_SIZE, h * HEAD_SIZE)
                for t in range(0, rows, TILE):
                    at = slice(t, t + TILE)
                    acc, m, l = extend(q_ref, acc_in, m_in, l_in, at, cols, k, v_ext)
                    acc_ref[at, cols] = acc
                    m_ref[at, cols] = m
                    l_ref[at, cols] = l

        each_group(groups, body)

    if len(lives) == 1:
        pl.when(live[0])(lambda: run(lambda g: [pair(kv_refs[0], g)]))
        return
    a, b = live

    def chosen(g):
        ka, va = pair(kv_refs[0], g)
        kb, vb = pair(kv_refs[1], g)
        return [(jnp.where(a, ka, kb), jnp.where(a, va, vb))]

    pl.when(a & b)(lambda: run(lambda g: [pair(r, g) for r in kv_refs]))
    pl.when(a ^ b)(lambda: run(chosen))


def last_kernel(
    heads, groups, alive, at_ref, q_ref, kv_ref, acc_in, m_in, l_in, side_ref, gain_ref, comb_ref, sq_ref
):
    d = HEAD_SIZE
    rows = q_ref.shape[0]
    live = alive(at_ref)
    sq_ref[...] = jnp.zeros_like(sq_ref)

    def run(update):
        def body(g):
            if update:
                k, v_ext = joined([pair(kv_ref, g)])
            for t in range(0, rows, TILE):
                at = slice(t, t + TILE)
                total = jnp.zeros((TILE, d), jnp.float32)
                for h in range(heads):
                    cols = span(g, heads * d, h * d)
                    if update:
                        acc, _, l = extend(q_ref, acc_in, m_in, l_in, at, cols, k, v_ext)
                    else:
                        acc, l = acc_in[at, cols], l_in[at, cols]
                    c = gain_ref[0:1, cols] * (side_ref[at, cols] + acc / l)
                    comb_ref[at, cols] = c
                    total = total + c * c
                sq_ref[:, at] += lax.dot_general(
                    jnp.ones((8, d), jnp.float32), total, nt_dims, precision=exact
                )

        each_group(groups, body)

    pl.when(live)(lambda: run(True))
    pl.when(jnp.logical_not(live))(lambda: run(False))


def weights_of(idx_ref, table_ref):
    entries = table_ref.shape[0]
    rows = idx_ref.shape[0]
    one_hot = (idx_ref[...] == lax.broadcasted_iota(jnp.int32, (rows, entries), 1)).astype(
        jnp.float32
    )
    return jnp.dot(one_hot, table_ref[...], precision=exact, preferred_element_type=jnp.float32)


def intra_kernel(heads, groups, levels, q_ref, k_ref, v_ref, idx_ref, table_ref, out_ref, w_ref):
    d = HEAD_SIZE
    rows = q_ref.shape[0]
    w_ref[...] = weights_of(idx_ref, table_ref)
    row = lax.broadcasted_iota(jnp.int32, (TILE, TILE), 0)
    col = lax.broadcasted_iota(jnp.int32, (TILE, TILE), 1)
    for g in range(groups):
        kv = slice(g * d, (g + 1) * d)
        for h in range(heads):
            head = g * heads + h
            cols = slice(head * d, (head + 1) * d)
            for t in range(0, rows, TILE):
                at = slice(t, t + TILE)
                a = scores_of(q_ref[at, cols], k_ref[: t + TILE, kv]) * (d * rows) ** (-0.5)
                tail = jnp.where(col <= row, a[:, t:], 0.0)
                a = jnp.concatenate([a[:, :t], tail], axis=1) if t else tail
                intra = jnp.dot(
                    a.astype(jnp.bfloat16),
                    v_ref[: t + TILE, kv],
                    preferred_element_type=jnp.float32,
                )
                lane = head * (levels + 1)
                out_ref[at, cols] = w_ref[at, lane : lane + 1] * intra


def readout_kernel(heads, groups, levels, at_ref, q_ref, w_ref, *refs):
    d = HEAD_SIZE
    buckets = refs[:levels]
    side_in, side_ref = refs[levels:]
    rows = q_ref.shape[0]
    here = at_ref[0]
    scales = [
        ((here >> (level - 1)) & 1).astype(jnp.float32) * (d * rows * 2 ** (level - 1)) ** (-0.5)
        for level in range(1, levels + 1)
    ]
    for g in range(groups):
        wide = jnp.concatenate([b[g] for b in buckets], axis=1)
        for h in range(heads):
            head = g * heads + h
            cols = slice(head * d, (head + 1) * d)
            for t in range(0, rows, TILE):
                at = slice(t, t + TILE)
                read = jnp.dot(q_ref[at, cols], wide, preferred_element_type=jnp.float32)
                out = side_in[at, cols]
                for level in range(levels):
                    lane = head * (levels + 1) + level + 1
                    out = out + (w_ref[at, lane : lane + 1] * scales[level]) * read[
                        :, level * d : (level + 1) * d
                    ]
                side_ref[at, cols] = out


def window_kernel(heads, groups, behind, at_ref, q_ref, own_ref, other_ref, *refs):
    d = HEAD_SIZE
    back = refs[:behind]
    side_in, side_ref = refs[behind:]
    rows = q_ref.shape[0]
    here = at_ref[0]
    pick = at_ref[1] != 0

    def run(general):
        def body(g):
            kx, vx = pair(back[-1], g)
            ky, vy = pair(other_ref, g)
            near = (jnp.where(pick, kx, ky), jnp.where(pick, vx, vy))
            k, v_ext = joined([pair(r, g) for r in back[:-1]] + [near, pair(own_ref, g)])
            for h in range(heads):
                cols = span(g, heads * d, h * d)
                for t in range(0, rows, TILE):
                    at = slice(t, t + TILE)
                    start = 0 if general else behind * rows + t - W
                    stop = behind * rows + rows if general else behind * rows + t + TILE
                    s = scores_of(q_ref[at, cols], k[start:stop])
                    if general:
                        at_row = behind * rows + t + lax.broadcasted_iota(jnp.int32, s.shape, 0)
                        at_col = lax.broadcasted_iota(jnp.int32, s.shape, 1)
                        allowed = (at_col <= at_row) & (at_col > at_row - W)
                        allowed = allowed & (at_col >= (behind - here) * rows)
                        s = jnp.where(allowed, s, far_below)
                    else:
                        s = lower_mask(s, True, True)
                    m = jnp.max(s, axis=1, keepdims=True) * UNIT
                    p = jnp.exp2(s * UNIT - m)
                    pv = jnp.dot(
                        p.astype(jnp.bfloat16), v_ext[start:stop], preferred_element_type=jnp.float32
                    )
                    side_ref[at, cols] = side_in[at, cols] + pv[:, :d] / pv[:, d:]

        each_group(groups, body)

    if behind * rows == W:
        pl.when(here >= behind)(lambda: run(False))
        pl.when(here < behind)(lambda: run(True))
    else:
        run(True)


def norm_kernel(columns, parts, comb_ref, *refs):
    sums = refs[0][...]
    for r in refs[1:parts]:
        sums = sums + r[...]
    out_ref = refs[parts]
    g = pl.program_id(0)
    wide = out_ref.shape[1]
    inv = lax.rsqrt(jnp.transpose(sums)[:, 0:1] / columns + 1e-06)
    out_ref[...] = (comb_ref[:, pl.ds(pl.multiple_of(g * wide, LANES), wide)] * inv).astype(
        out_ref.dtype
    )


def per_device(
    q_win,
    k_win,
    v_win,
    q_lin,
    k_lin,
    v_lin,
    level_table,
    level_index,
    q_cross,
    k_shared,
    v_shared,
    head_gain,
):
    d = HEAD_SIZE
    bf16, f32 = jnp.bfloat16, jnp.float32
    rows = q_win.shape[0]
    groups = k_win.shape[1] // d
    heads = q_win.shape[1] // k_win.shape[1]
    count = lax.axis_size("ctx")
    levels = count.bit_length() - 1
    here = lax.axis_index("ctx").astype(jnp.int32)
    behind = -(-W // rows)
    fixed = count == 8 and behind == 2

    full = jax.ShapeDtypeStruct((rows, q_win.shape[1]), f32)
    kv_type = jax.ShapeDtypeStruct((2, rows, k_win.shape[1]), bf16)

    def call(kernel, args, outs, alias=None, scalars=0, work=0.0, limit=24):
        keys = work * rows * rows * groups * heads
        return pl.pallas_call(
            kernel,
            in_specs=[SMEM] * scalars + [VMEM] * (len(args) - scalars),
            out_specs=[VMEM] * len(outs),
            out_shape=outs,
            input_output_aliases=alias or {},
            compiler_params=pltpu.CompilerParams(vmem_limit_bytes=limit << 20),
            cost_estimate=pl.CostEstimate(
                flops=int(4 * keys * d) + 1024, transcendentals=int(keys), bytes_accessed=1 << 20
            ),
        )(*args)

    part = functools.partial
    at = jnp.stack([here, here & 1])
    (shared,) = call(pack_kernel, [k_shared, v_shared], [kv_type])
    (near,) = call(pack_kernel, [k_win, v_win], [kv_type])
    state, half = call(
        state_kernel, [k_lin, v_lin], [jax.ShapeDtypeStruct((groups, d, d), t) for t in (f32, bf16)]
    )
    buckets = []
    for level in range(levels):
        arrived = partner(half, "ctx", level)
        buckets.append(arrived)
        state = state + arrived.astype(f32)
        half = state.astype(bf16)

    index = level_index.reshape(rows, 1)
    table = level_table.reshape(level_table.shape[0], -1)
    gain = jnp.repeat(head_gain, d).reshape(1, -1)

    kernel = lambda f, *extra: part(f, heads, groups, *extra)
    carry = tuple(call(kernel(local_kernel), [q_cross, shared], [full] * 3, work=0.75))
    side, weights = call(
        kernel(intra_kernel, levels),
        [q_lin, k_lin, v_lin, index, table],
        [full, jax.ShapeDtypeStruct((rows, table.shape[1]), f32)],
        work=0.75,
    )

    def piece(lives, kvs, carry, where=at):
        n = len(kvs) + 2
        return tuple(
            call(
                kernel(piece_kernel, lives),
                [where, q_cross, *kvs, *carry],
                [full] * 3,
                alias={n: 0, n + 1: 1, n + 2: 2},
                scalars=1,
                work=len(kvs),
            )
        )

    def windowed(side, back, other, flags):
        return call(
            kernel(window_kernel, behind),
            [flags, q_win, near, other, *back, side],
            [full],
            alias={4 + behind: 0},
            scalars=1,
            work=2.5,
        )[0]

    def read(side):
        return call(
            kernel(readout_kernel, levels),
            [at, q_lin, weights, *buckets, side],
            [full],
            alias={3 + levels: 0},
            scalars=1,
            work=0.75,
        )[0]

    def last(alive, kv, carry, side):
        return call(
            kernel(last_kernel, alive),
            [at, q_cross, kv, *carry, side, gain],
            [full, jax.ShapeDtypeStruct((8, rows), f32)],
            alias={6: 0},
            scalars=1,
            work=1,
        )

    if fixed:

        def straight(steps):
            return lambda ref: ref[0] >= 2 * steps

        def across(steps):
            return lambda ref: (ref[0] >= 2 * steps) if steps else (ref[1] == 1)

        sides = [(2 * i, 2 * i + 1) for i in range(count // 2)]
        z1 = shifted(shared, "ctx", 2)
        x0 = partner(shared, "ctx", 0)
        w2 = shifted(near, "ctx", 2)
        wx = lax.ppermute(near, "ctx", sides)
        z3 = shifted(shared, "ctx", 6)
        z2 = shifted(z1, "ctx", 2)
        x1 = partner(z1, "ctx", 0)
        wb = lax.ppermute(w2, "ctx", [(b, a) for a, b in sides])
        x3 = partner(z3, "ctx", 0)
        x2 = partner(z2, "ctx", 0)
        carry = piece([across(0), straight(1)], [x0, z1], carry)
        carry = piece([across(1), straight(3)], [x1, z3], carry)
        side = windowed(side, [w2, wx], wb, at)
        carry = piece([across(3), straight(2)], [x3, z2], carry)
        side = read(side)
        comb, sq = last(across(2), x2, carry, side)
    else:
        back = [shifted(near, "ctx", step) for step in range(behind, 0, -1)]
        side = read(windowed(side, back, back[-1], jnp.stack([here, here * 0 + 1])))
        every = lax.all_gather(shared, "ctx", axis=0, tiled=False)

        def step(source, carried):
            return piece(
                [lambda ref: ref[1] < ref[0]], [every[source]], carried, jnp.stack([here, source])
            )

        carry = lax.fori_loop(0, count - 2, step, carry)
        comb, sq = last(lambda ref: ref[0] > count - 2, every[count - 2], carry, side)

    members = lax.axis_size("head")
    if members & (members - 1) == 0:
        sums = [sq] + [
            lax.ppermute(sq, "head", [(i, i ^ k) for i in range(members)])
            for k in range(1, members)
        ]
    else:
        sums = [lax.psum(sq, "head")]
    return pl.pallas_call(
        part(norm_kernel, QH * d, len(sums)),
        grid=(groups,),
        in_specs=[VMEM] * (1 + len(sums)),
        out_specs=pl.BlockSpec((rows, heads * d), lambda g: (0, g)),
        out_shape=jax.ShapeDtypeStruct(q_win.shape, bf16),
        compiler_params=pltpu.CompilerParams(vmem_limit_bytes=12 << 20),
        name="norm",
    )(comb, *sums)


def solution(mesh):
    return jax.shard_map(
        per_device,
        mesh=mesh,
        in_specs=(
            P("ctx", "head"),
            P("ctx", "head"),
            P("ctx", "head"),
            P("ctx", "head"),
            P("ctx", "head"),
            P("ctx", "head"),
            P(None, "head", None),
            P("ctx"),
            P("ctx", "head"),
            P("ctx", "head"),
            P("ctx", "head"),
            P("head"),
        ),
        out_specs=P("ctx", "head"),
        check_vma=False,
    )
```

time: 188 us -> 124 us (0.66)
  the two profiles are of different devices: /device:TPU:30 before, /device:TPU:25 now
where the time goes in v2:
time: 124 us; the launch traced here: 123 us
  waiting for transfers between devices  45.2 us (36%)
  Pallas kernels  41.7 us (34%)
  starting transfers between devices  22.4 us (18%)
  local copies, waits for them, and re-layouts  12.4 us (10%)
    pallas_call x11, Pallas kernels, call(): pl.pallas_call(kernel, in_specs=[SMEM] * scalars + [VMEM] * (len(args) -...  39.5 us
    ppermute x7, waiting for transfers between devices, partner(): return lax.ppermute(block, axis, route)  37.3 us
    unnamed x28, local copies, waits for them, and re-layouts  9.36 us
    ppermute x7, starting transfers between devices, partner(): return lax.ppermute(block, axis, route)  7.56 us
    ppermute x4, starting transfers between devices, shifted(): lax.ppermute(value, axis, [(source, source + steps) for source in range(f...  5.28 us
    ppermute x4, waiting for transfers between devices, shifted(): lax.ppermute(value, axis, [(source, source + steps) for source in range(f...  5.22 us
    ppermute x3, starting transfers between devices, per_device(): lax.ppermute(sq, 'head', [(i, i ^ k) for i in range(members)])  4.38 us
    ppermute x1, starting transfers between devices, per_device(): wx = lax.ppermute(near, 'ctx', sides)  3.9 us
  transfers between devices with their start and end apart: 16, of which 5 were waited for; matrix products, arithmetic and copies ran while one was open for 3% of the time, Pallas kernels for 27%

profile of v2, /device:TPU:25, one launch (start us, length us, event | category | flops | bytes accessed | tf_op | source)
XLA Modules:
  0.0 122.9 jit_solution(6032822168850242421)
XLA Ops:
  0.0 1.0 copy-done.8
  1.0 0.9 copy-done.9
  2.0 0.0 copy-start.1
  2.0 1.4 %collective-permute-start = (bf16[2,256,512]{2,1,0:T(8,128)(2,1)S(1)}, bf16[2,256,512]{2,1,0:T(8,128)(2,1)}, u32[]{:S(2)}, u32[]{:S(2)}) collective-permute-start(bf16[2,256,512]{2,1,0:T(8,128)(2,1)S(1)} %shard_map.118.kv_ref), channel_id=1, source_target_pairs={{0,8},{4,12},{8,16},{12,20},{16,24},{20,28},{1,9},{5,13},{9,17},{1... | collective-permute-start | bytes 1572872 | tf_op jit(solution)/shard_map/ppermute | solution.py:24
  3.5 0.0 copy-start.2
  3.5 0.9 copy-done.2
  4.4 0.9 copy-done.4
  5.4 0.3 shard_map.124
  5.6 1.3 %collective-permute-start.7 = (bf16[4,128,128]{2,1,0:T(8,128)(2,1)S(1)}, bf16[4,128,128]{2,1,0:T(8,128)(2,1)S(1)}, u32[]{:S(2)}, u32[]{:S(2)}) collective-permute-start(bf16[4,128,128]{2,1,0:T(8,128)(2,1)S(1)} %get-tuple-element.36), channel_id=1, source_target_pairs={{0,4},{4,0},{8,12},{12,8},{16,20},{20,16},{24,28},{28,24},{1,5},{5... | collective-permute-start | bytes 393224 | tf_op jit(solution)/shard_map/ppermute | solution.py:34
  6.9 0.9 copy-done.10
  7.9 0.9 copy-done.11
  8.9 1.3 %collective-permute-start.10 = (bf16[2,256,512]{2,1,0:T(8,128)(2,1)S(1)}, bf16[2,256,512]{2,1,0:T(8,128)(2,1)}, u32[]{:S(2)}, u32[]{:S(2)}) collective-permute-start(bf16[2,256,512]{2,1,0:T(8,128)(2,1)S(1)} %shard_map.125.own_ref), channel_id=1, source_target_pairs={{0,8},{4,12},{8,16},{12,20},{16,24},{20,28},{1,9},{5,13},{9,17},{1... | collective-permute-start | bytes 1572872 | tf_op jit(solution)/shard_map/ppermute | solution.py:24
  10.2 0.3 collective-permute-start.6
  10.5 1.3 %collective-permute-start.3 = (bf16[2,256,512]{2,1,0:T(8,128)(2,1)S(1)}, bf16[2,256,512]{2,1,0:T(8,128)(2,1)}, u32[]{:S(2)}, u32[]{:S(2)}) collective-permute-start(bf16[2,256,512]{2,1,0:T(8,128)(2,1)S(1)} %shard_map.118.kv_ref), channel_id=1, source_target_pairs={{0,24},{4,28},{1,25},{5,29},{2,26},{6,30},{3,27},{7,31}} | collective-permute-start | bytes 1572872 | tf_op jit(solution)/shard_map/ppermute | solution.py:24
  11.8 5.2 %collective-permute-done.refs_1_ = bf16[2,256,512]{2,1,0:T(8,128)(2,1)} collective-permute-done((bf16[2,256,512]{2,1,0:T(8,128)(2,1)S(1)}, bf16[2,256,512]{2,1,0:T(8,128)(2,1)}, u32[]{:S(2)}, u32[]{:S(2)}) %collective-permute-start) | collective-permute-done | bytes 524320 | tf_op jit(solution)/shard_map/ppermute | solution.py:24
  17.0 1.3 %collective-permute-start.1 = (bf16[2,256,512]{2,1,0:T(8,128)(2,1)}, bf16[2,256,512]{2,1,0:T(8,128)(2,1)}, u32[]{:S(2)}, u32[]{:S(2)}) collective-permute-start(bf16[2,256,512]{2,1,0:T(8,128)(2,1)} %collective-permute-done.refs_1_), channel_id=1, source_target_pairs={{0,8},{4,12},{8,16},{12,20},{16,24},{20,28},{1,9},{5,13},{9,17},{1... | collective-permute-start | bytes 1572872 | tf_op jit(solution)/shard_map/ppermute | solution.py:24
  18.3 0.0 collective-permute-done.7.refs_0_
  18.3 2.1 %collective-permute-start.8 = (bf16[4,128,128]{2,1,0:T(8,128)(2,1)S(1)}, bf16[4,128,128]{2,1,0:T(8,128)(2,1)}, u32[]{:S(2)}, u32[]{:S(2)}) collective-permute-start(bf16[4,128,128]{2,1,0:T(8,128)(2,1)S(1)} %fusion), channel_id=1, source_target_pairs={{0,8},{8,0},{4,12},{12,4},{16,24},{24,16},{20,28},{28,20},{1,9},{9... | collective-permute-start | bytes 393224 | tf_op jit(solution)/shard_map/ppermute | solution.py:34
  20.5 33.0 %collective-permute-done.8.refs_1_ = bf16[4,128,128]{2,1,0:T(8,128)(2,1)} collective-permute-done((bf16[4,128,128]{2,1,0:T(8,128)(2,1)S(1)}, bf16[4,128,128]{2,1,0:T(8,128)(2,1)}, u32[]{:S(2)}, u32[]{:S(2)}) %collective-permute-start.8) | collective-permute-done | bytes 131104 | tf_op jit(solution)/shard_map/ppermute | solution.py:34
  53.5 3.9 %collective-permute-start.12 = (bf16[2,256,512]{2,1,0:T(8,128)(2,1)S(1)}, bf16[2,256,512]{2,1,0:T(8,128)(2,1)}, u32[]{:S(2)}, u32[]{:S(2)}) collective-permute-start(bf16[2,256,512]{2,1,0:T(8,128)(2,1)S(1)} %shard_map.125.own_ref), channel_id=1, source_target_pairs={{0,4},{8,12},{16,20},{24,28},{1,5},{9,13},{17,21},{25,29},{2,6},{1... | collective-permute-start | bytes 1572872 | tf_op jit(solution)/shard_map/ppermute | solution.py:453
  57.4 1.5 %copy.26.idx_ref = s32[256,1]{1,0:T(8,128)} copy(s32[256,1]{0,1:T(1,128)} %bitcast.7) | data formatting | bytes 2048 | tf_op jit(solution)/shard_map/reshape | solution.py:385
  58.9 1.4 %copy.27.table_ref = f32[64,64]{1,0:T(8,128)} copy(f32[64,64]{0,1:T(8,128)} %bitcast.6) | data formatting | bytes 32768 | tf_op jit(solution)/shard_map/reshape | solution.py:386
  60.3 0.0 collective-permute-done.10.refs_0_
  60.3 1.3 %collective-permute-start.11 = (bf16[2,256,512]{2,1,0:T(8,128)(2,1)}, bf16[2,256,512]{2,1,0:T(8,128)(2,1)S(1)}, u32[]{:S(2)}, u32[]{:S(2)}) collective-permute-start(bf16[2,256,512]{2,1,0:T(8,128)(2,1)} %collective-permute-done.10.refs_0_), channel_id=1, source_target_pairs={{4,0},{12,8},{20,16},{28,24},{5,1},{13,9},{21,17},{29,25},{6,2},{1... | collective-permute-start | bytes 1572872 | tf_op jit(solution)/shard_map/ppermute | solution.py:457
  61.6 0.0 copy-done
  61.6 3.4 %shard_map.119 = (f32[256,2048]{1,0:T(8,128)S(1)}, f32[256,2048]{1,0:T(8,128)S(1)}, f32[256,2048]{1,0:T(8,128)S(1)}) custom-call(bf16[256,2048]{1,0:T(8,128)(2,1)S(1)} %copy-done, bf16[2,256,512]{2,1,0:T(8,128)(2,1)S(1)} %shard_map.118.kv_ref), custom_call_target="tpu_custom_call" | custom-call | flops 402654208 | bytes 1048576 | tf_op jit(solution)/shard_map/pallas_call | solution.py:359
  65.0 0.1 pad_add_fusion.at_ref
  65.1 0.0 collective-permute-done.6.refs_0_
  65.1 2.1 %collective-permute-start.5 = (bf16[2,256,512]{2,1,0:T(8,128)(2,1)}, bf16[2,256,512]{2,1,0:T(8,128)(2,1)S(1)}, u32[]{:S(2)}, u32[]{:S(2)}) collective-permute-start(bf16[2,256,512]{2,1,0:T(8,128)(2,1)} %collective-permute-done.refs_1_), channel_id=1, source_target_pairs={{0,4},{4,0},{8,12},{12,8},{16,20},{20,16},{24,28},{28,24},{1,5},{5... | collective-permute-start | bytes 1572872 | tf_op jit(solution)/shard_map/ppermute | solution.py:34
  67.2 0.0 copy-done.1
  67.2 0.9 copy-done.3
  68.2 0.9 copy-done.5
  69.1 0.9 copy-done.7
  70.0 0.8 copy-done.12
  70.8 3.3 %shard_map.123 = (f32[256,2048]{1,0:T(8,128)S(1)}, f32[256,64]{1,0:T(8,128)S(1)}) custom-call(bf16[256,2048]{1,0:T(8,128)(2,1)S(1)} %copy-done.1, bf16[256,512]{1,0:T(8,128)(2,1)S(1)} %copy-done.3, bf16[256,512]{1,0:T(8,128)(2,1)S(1)} %copy-done.5, s32[256,1]{1,0:T(8,128)S(1)} %copy-done.7, f32[64,64]{1,0:T(8,128)S(1)} %copy-done.12), custom_call_target="tpu_custom_call" | custom-call | flops 402654208 | bytes 1048576 | tf_op jit(solution)/shard_map/pallas_call | solution.py:359
  74.1 0.0 collective-permute-done.3.refs_1_
  74.1 0.1 collective-permute-start.4
  74.2 0.0 collective-permute-done.1.refs_1_
  74.2 1.4 %collective-permute-start.2 = (bf16[2,256,512]{2,1,0:T(8,128)(2,1)}, bf16[2,256,512]{2,1,0:T(8,128)(2,1)S(1)}, u32[]{:S(2)}, u32[]{:S(2)}) collective-permute-start(bf16[2,256,512]{2,1,0:T(8,128)(2,1)} %collective-permute-done.1.refs_1_), channel_id=1, source_target_pairs={{0,4},{4,0},{8,12},{12,8},{16,20},{20,16},{24,28},{28,24},{1,5},{5... | collective-permute-start | bytes 1572872 | tf_op jit(solution)/shard_map/ppermute | solution.py:34
  75.7 1.0 add_convert_fusion
  76.6 0.0 collective-permute-done.12.refs_1_
  76.6 0.2 collective-permute-start.9
  76.8 4.3 %shard_map.120 = (f32[256,2048]{1,0:T(8,128)S(1)}, f32[256,2048]{1,0:T(8,128)S(1)}, f32[256,2048]{1,0:T(8,128)S(1)}) custom-call(s32[2]{0:T(128)S(1)} %pad_add_fusion.at_ref, bf16[256,2048]{1,0:T(8,128)(2,1)S(1)} %copy-done, bf16[2,256,512]{2,1,0:T(8,128)(2,1)} %collective-permute-done.6.refs_0_, ...), custom_call_target="tpu_custom_call", output_to_operand_aliasing={{0}: (4, {}), {1}: (5, {}), {2}: (6, {})} | custom-call | flops 1073742848 | bytes 1048576 | tf_op jit(solution)/shard_map/pallas_call | solution.py:359
  81.0 0.0 collective-permute-done.11.other_ref
  81.1 0.0 copy-done.6
  81.1 7.5 %shard_map.126.refs_3_ = f32[256,2048]{1,0:T(8,128)S(1)} custom-call(s32[2]{0:T(128)S(1)} %pad_add_fusion.at_ref, bf16[256,2048]{1,0:T(8,128)(2,1)S(1)} %copy-done.6, bf16[2,256,512]{2,1,0:T(8,128)(2,1)S(1)} %shard_map.125.own_ref, bf16[2,256,512]{2,1,0:T(8,128)(2,1)S(1)} %collective-permute-done.11.other_ref, ...), custom_call_target="tpu_custom_call", output_to_operand_aliasing={{}: (6, {})} | custom-call | flops 1342178304 | bytes 1048576 | tf_op jit(solution)/shard_map/pallas_call | solution.py:359
  88.6 0.0 collective-permute-done.9.refs_2_
  88.6 3.2 %shard_map.127.side_ref = f32[256,2048]{1,0:T(8,128)S(1)} custom-call(s32[2]{0:T(128)S(1)} %pad_add_fusion.at_ref, bf16[256,2048]{1,0:T(8,128)(2,1)S(1)} %copy-done.1, f32[256,64]{1,0:T(8,128)S(1)} %get-tuple-element.35.w_ref, bf16[4,128,128]{2,1,0:T(8,128)(2,1)S(1)} %collective-permute-done.7.refs_0_, ...), custom_call_target="tpu_custom_call", output_to_operand_aliasing={{}: (6, {})} | custom-call | flops 402654208 | bytes 1048576 | tf_op jit(solution)/shard_map/pallas_call | solution.py:359
  91.8 0.0 collective-permute-done.5.refs_0_
  91.8 5.9 %shard_map.121 = (f32[256,2048]{1,0:T(8,128)S(1)}, f32[256,2048]{1,0:T(8,128)S(1)}, f32[256,2048]{1,0:T(8,128)S(1)}) custom-call(s32[2]{0:T(128)S(1)} %pad_add_fusion.at_ref, bf16[256,2048]{1,0:T(8,128)(2,1)S(1)} %copy-done, bf16[2,256,512]{2,1,0:T(8,128)(2,1)S(1)} %collective-permute-done.5.refs_0_, ...), custom_call_target="tpu_custom_call", output_to_operand_aliasing={{0}: (4, {}), {1}: (5, {}), {2}: (6, {})} | custom-call | flops 1073742848 | bytes 1048576 | tf_op jit(solution)/shard_map/pallas_call | solution.py:359
  97.8 0.0 collective-permute-done.4.refs_0_
  97.8 0.0 copy-start.13
  97.8 5.7 %shard_map.122 = (f32[256,2048]{1,0:T(8,128)S(1)}, f32[256,2048]{1,0:T(8,128)S(1)}, f32[256,2048]{1,0:T(8,128)S(1)}) custom-call(s32[2]{0:T(128)S(1)} %pad_add_fusion.at_ref, bf16[256,2048]{1,0:T(8,128)(2,1)S(1)} %copy-done, bf16[2,256,512]{2,1,0:T(8,128)(2,1)S(1)} %collective-permute-done.4.refs_0_, ...), custom_call_target="tpu_custom_call", output_to_operand_aliasing={{0}: (4, {}), {1}: (5, {}), {2}: (6, {})} | custom-call | flops 1073742848 | bytes 1048576 | tf_op jit(solution)/shard_map/pallas_call | solution.py:359
  103.5 4.3 %collective-permute-done.2.kv_ref = bf16[2,256,512]{2,1,0:T(8,128)(2,1)S(1)} collective-permute-done((bf16[2,256,512]{2,1,0:T(8,128)(2,1)}, bf16[2,256,512]{2,1,0:T(8,128)(2,1)S(1)}, u32[]{:S(2)}, u32[]{:S(2)}) %collective-permute-start.2) | collective-permute-done | bytes 524320 | tf_op jit(solution)/shard_map/ppermute | solution.py:34
  107.8 0.0 copy-done.13
  107.8 0.1 broadcast_in_dim.3
  107.9 5.8 %shard_map.128 = (f32[256,2048]{1,0:T(8,128)S(1)}, f32[8,256]{1,0:T(8,128)S(1)}) custom-call(s32[2]{0:T(128)S(1)} %pad_add_fusion.at_ref, bf16[256,2048]{1,0:T(8,128)(2,1)S(1)} %copy-done, bf16[2,256,512]{2,1,0:T(8,128)(2,1)S(1)} %collective-permute-done.2.kv_ref, f32[256,2048]{1,0:T(8,128)S(1)} %get-tuple-element.32.acc_in, ...), custom_call_target="tpu_custom_call", output_to_operand_aliasing={{0}: (6, {})} | custom-call | flops 536871936 | bytes 1048576 | tf_op jit(solution)/shard_map/pallas_call | solution.py:359
  113.7 2.7 %collective-permute-start.13 = (f32[8,256]{1,0:T(8,128)S(1)}, f32[8,256]{1,0:T(8,128)S(1)}, u32[]{:S(2)}, u32[]{:S(2)}) collective-permute-start(f32[8,256]{1,0:T(8,128)S(1)} %get-tuple-element.40.refs_0_), channel_id=1, source_target_pairs={{0,1},{1,0},{2,3},{3,2},{4,5},{5,4},{6,7},{7,6},{8,9},{9,8},{10,11... | collective-permute-start | bytes 24584 | tf_op jit(solution)/shard_map/ppermute | solution.py:482
  116.4 1.2 %collective-permute-start.14 = (f32[8,256]{1,0:T(8,128)S(1)}, f32[8,256]{1,0:T(8,128)S(1)}, u32[]{:S(2)}, u32[]{:S(2)}) collective-permute-start(f32[8,256]{1,0:T(8,128)S(1)} %get-tuple-element.40.refs_0_), channel_id=1, source_target_pairs={{0,2},{1,3},{2,0},{3,1},{4,6},{5,7},{6,4},{7,5},{8,10},{9,11},{10,... | collective-permute-start | bytes 24584 | tf_op jit(solution)/shard_map/ppermute | solution.py:482
  117.6 0.4 collective-permute-start.15
  118.0 0.0 collective-permute-done.13.refs_1_
  118.1 0.8 collective-permute-done.14.refs_2_
  118.9 1.8 %collective-permute-done.15.refs_3_ = f32[8,256]{1,0:T(8,128)S(1)} collective-permute-done((f32[8,256]{1,0:T(8,128)S(1)}, f32[8,256]{1,0:T(8,128)S(1)}, u32[]{:S(2)}, u32[]{:S(2)}) %collective-permute-start.15) | collective-permute-done | bytes 8224 | tf_op jit(solution)/shard_map/ppermute | solution.py:482
  120.7 2.2 %norm.1 = bf16[256,2048]{1,0:T(8,128)(2,1)} custom-call(f32[256,2048]{1,0:T(8,128)S(1)} %get-tuple-element.39.comb_ref, f32[8,256]{1,0:T(8,128)S(1)} %get-tuple-element.40.refs_0_, f32[8,256]{1,0:T(8,128)S(1)} %collective-permute-done.13.refs_1_, f32[8,256]{1,0:T(8,128)S(1)} %collective-permute-done.14.refs_2_, f32[8,256]{1,0:T(8,128)S(1)} %collective-permute-done.15.refs_3_), custom_call_target="tpu_custom_call" | custom-call | tf_op jit(solution)/shard_map/norm/pallas_call | solution.py:487
  (14 shorter events, 0.1 us)
Async XLA Ops:
  0.0 61.6 %copy-start = (bf16[256,2048]{1,0:T(8,128)(2,1)S(1)}, bf16[256,2048]{1,0:T(8,128)(2,1)}, u32[]{:S(2)}) copy-start(bf16[256,2048]{1,0:T(8,128)(2,1)} %q_ref.15) | copy-start | bytes 3145732
  0.0 1.0 copy-start.8
  1.0 0.9 copy-start.9
  2.0 65.2 %copy-start.1 = (bf16[256,2048]{1,0:T(8,128)(2,1)S(1)}, bf16[256,2048]{1,0:T(8,128)(2,1)}, u32[]{:S(2)}) copy-start(bf16[256,2048]{1,0:T(8,128)(2,1)} %q_ref.14) | copy-start | bytes 3145732
  2.0 14.9 %collective-permute-start = (bf16[2,256,512]{2,1,0:T(8,128)(2,1)S(1)}, bf16[2,256,512]{2,1,0:T(8,128)(2,1)}, u32[]{:S(2)}, u32[]{:S(2)}) collective-permute-start(bf16[2,256,512]{2,1,0:T(8,128)(2,1)S(1)} %shard_map.118.kv_ref), channel_id=1, source_target_pairs={{0,8},{4,12},{8,16},{12,20},{16,24},{20,28},{1,9},{5,13},{9,17},{1... | collective-permute-start | bytes 1572872 | tf_op jit(solution)/shard_map/ppermute | solution.py:24
  3.5 1.0 copy-start.2
  4.4 0.9 copy-start.4
  5.6 12.6 %collective-permute-start.7 = (bf16[4,128,128]{2,1,0:T(8,128)(2,1)S(1)}, bf16[4,128,128]{2,1,0:T(8,128)(2,1)S(1)}, u32[]{:S(2)}, u32[]{:S(2)}) collective-permute-start(bf16[4,128,128]{2,1,0:T(8,128)(2,1)S(1)} %get-tuple-element.36), channel_id=1, source_target_pairs={{0,4},{4,0},{8,12},{12,8},{16,20},{20,16},{24,28},{28,24},{1,5},{5... | collective-permute-start | bytes 393224 | tf_op jit(solution)/shard_map/ppermute | solution.py:34
  6.9 0.9 copy-start.10
  7.9 0.9 copy-start.11
  8.9 51.5 %collective-permute-start.10 = (bf16[2,256,512]{2,1,0:T(8,128)(2,1)S(1)}, bf16[2,256,512]{2,1,0:T(8,128)(2,1)}, u32[]{:S(2)}, u32[]{:S(2)}) collective-permute-start(bf16[2,256,512]{2,1,0:T(8,128)(2,1)S(1)} %shard_map.125.own_ref), channel_id=1, source_target_pairs={{0,8},{4,12},{8,16},{12,20},{16,24},{20,28},{1,9},{5,13},{9,17},{1... | collective-permute-start | bytes 1572872 | tf_op jit(solution)/shard_map/ppermute | solution.py:24
  10.2 54.9 %collective-permute-start.6 = (bf16[2,256,512]{2,1,0:T(8,128)(2,1)S(1)}, bf16[2,256,512]{2,1,0:T(8,128)(2,1)}, u32[]{:S(2)}, u32[]{:S(2)}) collective-permute-start(bf16[2,256,512]{2,1,0:T(8,128)(2,1)S(1)} %shard_map.118.kv_ref), channel_id=1, source_target_pairs={{0,4},{4,0},{8,12},{12,8},{16,20},{20,16},{24,28},{28,24},{1,5},{5... | collective-permute-start | bytes 1572872 | tf_op jit(solution)/shard_map/ppermute | solution.py:34
  10.5 63.6 %collective-permute-start.3 = (bf16[2,256,512]{2,1,0:T(8,128)(2,1)S(1)}, bf16[2,256,512]{2,1,0:T(8,128)(2,1)}, u32[]{:S(2)}, u32[]{:S(2)}) collective-permute-start(bf16[2,256,512]{2,1,0:T(8,128)(2,1)S(1)} %shard_map.118.kv_ref), channel_id=1, source_target_pairs={{0,24},{4,28},{1,25},{5,29},{2,26},{6,30},{3,27},{7,31}} | collective-permute-start | bytes 1572872 | tf_op jit(solution)/shard_map/ppermute | solution.py:24
  17.0 57.2 %collective-permute-start.1 = (bf16[2,256,512]{2,1,0:T(8,128)(2,1)}, bf16[2,256,512]{2,1,0:T(8,128)(2,1)}, u32[]{:S(2)}, u32[]{:S(2)}) collective-permute-start(bf16[2,256,512]{2,1,0:T(8,128)(2,1)} %collective-permute-done.refs_1_), channel_id=1, source_target_pairs={{0,8},{4,12},{8,16},{12,20},{16,24},{20,28},{1,9},{5,13},{9,17},{1... | collective-permute-start | bytes 1572872 | tf_op jit(solution)/shard_map/ppermute | solution.py:24
  18.3 35.2 %collective-permute-start.8 = (bf16[4,128,128]{2,1,0:T(8,128)(2,1)S(1)}, bf16[4,128,128]{2,1,0:T(8,128)(2,1)}, u32[]{:S(2)}, u32[]{:S(2)}) collective-permute-start(bf16[4,128,128]{2,1,0:T(8,128)(2,1)S(1)} %fusion), channel_id=1, source_target_pairs={{0,8},{8,0},{4,12},{12,4},{16,24},{24,16},{20,28},{28,20},{1,9},{9... | collective-permute-start | bytes 393224 | tf_op jit(solution)/shard_map/ppermute | solution.py:34
  53.5 23.1 %collective-permute-start.12 = (bf16[2,256,512]{2,1,0:T(8,128)(2,1)S(1)}, bf16[2,256,512]{2,1,0:T(8,128)(2,1)}, u32[]{:S(2)}, u32[]{:S(2)}) collective-permute-start(bf16[2,256,512]{2,1,0:T(8,128)(2,1)S(1)} %shard_map.125.own_ref), channel_id=1, source_target_pairs={{0,4},{8,12},{16,20},{24,28},{1,5},{9,13},{17,21},{25,29},{2,6},{1... | collective-permute-start | bytes 1572872 | tf_op jit(solution)/shard_map/ppermute | solution.py:453
  60.3 20.7 %collective-permute-start.11 = (bf16[2,256,512]{2,1,0:T(8,128)(2,1)}, bf16[2,256,512]{2,1,0:T(8,128)(2,1)S(1)}, u32[]{:S(2)}, u32[]{:S(2)}) collective-permute-start(bf16[2,256,512]{2,1,0:T(8,128)(2,1)} %collective-permute-done.10.refs_0_), channel_id=1, source_target_pairs={{4,0},{12,8},{20,16},{28,24},{5,1},{13,9},{21,17},{29,25},{6,2},{1... | collective-permute-start | bytes 1572872 | tf_op jit(solution)/shard_map/ppermute | solution.py:457
  65.1 26.7 %collective-permute-start.5 = (bf16[2,256,512]{2,1,0:T(8,128)(2,1)}, bf16[2,256,512]{2,1,0:T(8,128)(2,1)S(1)}, u32[]{:S(2)}, u32[]{:S(2)}) collective-permute-start(bf16[2,256,512]{2,1,0:T(8,128)(2,1)} %collective-permute-done.refs_1_), channel_id=1, source_target_pairs={{0,4},{4,0},{8,12},{12,8},{16,20},{20,16},{24,28},{28,24},{1,5},{5... | collective-permute-start | bytes 1572872 | tf_op jit(solution)/shard_map/ppermute | solution.py:34
  67.2 1.0 copy-start.3
  68.2 0.9 copy-start.5
  69.1 0.9 copy-start.7
  70.0 0.8 copy-start.12
  74.1 23.6 %collective-permute-start.4 = (bf16[2,256,512]{2,1,0:T(8,128)(2,1)}, bf16[2,256,512]{2,1,0:T(8,128)(2,1)S(1)}, u32[]{:S(2)}, u32[]{:S(2)}) collective-permute-start(bf16[2,256,512]{2,1,0:T(8,128)(2,1)} %collective-permute-done.3.refs_1_), channel_id=1, source_target_pairs={{0,4},{4,0},{8,12},{12,8},{16,20},{20,16},{24,28},{28,24},{1,5},{5... | collective-permute-start | bytes 1572872 | tf_op jit(solution)/shard_map/ppermute | solution.py:34
  74.2 33.6 %collective-permute-start.2 = (bf16[2,256,512]{2,1,0:T(8,128)(2,1)}, bf16[2,256,512]{2,1,0:T(8,128)(2,1)S(1)}, u32[]{:S(2)}, u32[]{:S(2)}) collective-permute-start(bf16[2,256,512]{2,1,0:T(8,128)(2,1)} %collective-permute-done.1.refs_1_), channel_id=1, source_target_pairs={{0,4},{4,0},{8,12},{12,8},{16,20},{20,16},{24,28},{28,24},{1,5},{5... | collective-permute-start | bytes 1572872 | tf_op jit(solution)/shard_map/ppermute | solution.py:34
  76.6 12.0 %collective-permute-start.9 = (bf16[4,128,128]{2,1,0:T(8,128)(2,1)S(1)}, bf16[4,128,128]{2,1,0:T(8,128)(2,1)S(1)}, u32[]{:S(2)}, u32[]{:S(2)}) collective-permute-start(bf16[4,128,128]{2,1,0:T(8,128)(2,1)S(1)} %add_convert_fusion), channel_id=1, source_target_pairs={{0,16},{16,0},{4,20},{20,4},{8,24},{24,8},{12,28},{28,12},{1,17},{... | collective-permute-start | bytes 393224 | tf_op jit(solution)/shard_map/ppermute | solution.py:34
  76.8 4.3 %copy-start.6 = (bf16[256,2048]{1,0:T(8,128)(2,1)S(1)}, bf16[256,2048]{1,0:T(8,128)(2,1)}, u32[]{:S(2)}) copy-start(bf16[256,2048]{1,0:T(8,128)(2,1)} %q_ref.13) | copy-start | bytes 3145732
  97.8 10.0 %copy-start.13 = (f32[16]{0:T(128)S(1)}, f32[16]{0:T(128)}, u32[]{:S(2)}) copy-start(f32[16]{0:T(128)} %param.23) | copy-start | bytes 196
  113.7 4.4 %collective-permute-start.13 = (f32[8,256]{1,0:T(8,128)S(1)}, f32[8,256]{1,0:T(8,128)S(1)}, u32[]{:S(2)}, u32[]{:S(2)}) collective-permute-start(f32[8,256]{1,0:T(8,128)S(1)} %get-tuple-element.40.refs_0_), channel_id=1, source_target_pairs={{0,1},{1,0},{2,3},{3,2},{4,5},{5,4},{6,7},{7,6},{8,9},{9,8},{10,11... | collective-permute-start | bytes 24584 | tf_op jit(solution)/shard_map/ppermute | solution.py:482
  116.4 2.5 %collective-permute-start.14 = (f32[8,256]{1,0:T(8,128)S(1)}, f32[8,256]{1,0:T(8,128)S(1)}, u32[]{:S(2)}, u32[]{:S(2)}) collective-permute-start(f32[8,256]{1,0:T(8,128)S(1)} %get-tuple-element.40.refs_0_), channel_id=1, source_target_pairs={{0,2},{1,3},{2,0},{3,1},{4,6},{5,7},{6,4},{7,5},{8,10},{9,11},{10,... | collective-permute-start | bytes 24584 | tf_op jit(solution)/shard_map/ppermute | solution.py:482
  117.6 3.1 %collective-permute-start.15 = (f32[8,256]{1,0:T(8,128)S(1)}, f32[8,256]{1,0:T(8,128)S(1)}, u32[]{:S(2)}, u32[]{:S(2)}) collective-permute-start(f32[8,256]{1,0:T(8,128)S(1)} %get-tuple-element.40.refs_0_), channel_id=1, source_target_pairs={{0,3},{1,2},{2,1},{3,0},{4,7},{5,6},{6,5},{7,4},{8,11},{9,10},{10,... | collective-permute-start | bytes 24584 | tf_op jit(solution)/shard_map/ppermute | solution.py:482

commit v3 on v2

--- a/solution.py
+++ b/solution.py
@@ -16,6 +16,7 @@
 far_below = -1e30
 exact = lax.Precision.HIGHEST
 nt_dims = (((1,), (1,)), ((), ()))
+tn_dims = (((0,), (0,)), ((), ()))
 
 
 def shifted(value, axis, steps):
@@ -83,22 +84,16 @@
     return k, with_ones(v)
 
 
-def pack_kernel(k_ref, v_ref, out_ref):
-    out_ref[0] = k_ref[...]
-    out_ref[1] = v_ref[...]
-
-
-def state_kernel(k_ref, v_ref, wide_ref, half_ref):
-    for g in range(wide_ref.shape[0]):
-        cols = slice(g * HEAD_SIZE, (g + 1) * HEAD_SIZE)
-        state = lax.dot_general(
-            k_ref[:, cols],
-            v_ref[:, cols],
-            (((0,), (0,)), ((), ())),
-            preferred_element_type=jnp.float32,
-        )
-        wide_ref[g] = state
-        half_ref[g] = state.astype(half_ref.dtype)
+def fetched(copies, sem):
+    started = [pltpu.make_async_copy(src, dst, sem.at[i]) for i, (src, dst) in enumerate(copies)]
+    for c in started:
+        c.start()
+    return started
+
+
+def pack_kernel(k_ref, v_ref, out_ref, sem):
+    for c in fetched([(k_ref, out_ref.at[0]), (v_ref, out_ref.at[1])], sem):
+        c.wait()
 
 
 def local_kernel(heads, groups, q_ref, kv_ref, acc_ref, m_ref, l_ref):
@@ -208,33 +203,47 @@
 
 
 def weights_of(idx_ref, table_ref):
-    entries = table_ref.shape[0]
-    rows = idx_ref.shape[0]
-    one_hot = (idx_ref[...] == lax.broadcasted_iota(jnp.int32, (rows, entries), 1)).astype(
+    rows = idx_ref.shape[1]
+    entries = table_ref.shape[2]
+    one_hot = (idx_ref[...] == lax.broadcasted_iota(jnp.int32, (entries, rows), 0)).astype(
         jnp.float32
     )
-    return jnp.dot(one_hot, table_ref[...], precision=exact, preferred_element_type=jnp.float32)
-
-
-def intra_kernel(heads, groups, levels, q_ref, k_ref, v_ref, idx_ref, table_ref, out_ref, w_ref):
+    table = jnp.concatenate([table_ref[h] for h in range(table_ref.shape[0])], axis=0)
+    return jnp.transpose(
+        jnp.dot(table, one_hot, precision=exact, preferred_element_type=jnp.float32)
+    )
+
+
+def intra_kernel(
+    heads, groups, levels, k_ref, v_ref, q_ref, idx_ref, table_ref, *refs
+):
+    out_ref, w_ref, wide_ref, half_ref, kv_ref, sem = refs
     d = HEAD_SIZE
     rows = q_ref.shape[0]
+    moves = fetched([(k_ref, kv_ref.at[0]), (v_ref, kv_ref.at[1])], sem)
     w_ref[...] = weights_of(idx_ref, table_ref)
+    for c in moves:
+        c.wait()
     row = lax.broadcasted_iota(jnp.int32, (TILE, TILE), 0)
     col = lax.broadcasted_iota(jnp.int32, (TILE, TILE), 1)
     for g in range(groups):
         kv = slice(g * d, (g + 1) * d)
+        state = lax.dot_general(
+            kv_ref[0, :, kv], kv_ref[1, :, kv], tn_dims, preferred_element_type=jnp.float32
+        )
+        wide_ref[g] = state
+        half_ref[g] = state.astype(half_ref.dtype)
         for h in range(heads):
             head = g * heads + h
             cols = slice(head * d, (head + 1) * d)
             for t in range(0, rows, TILE):
                 at = slice(t, t + TILE)
-                a = scores_of(q_ref[at, cols], k_ref[: t + TILE, kv]) * (d * rows) ** (-0.5)
+                a = scores_of(q_ref[at, cols], kv_ref[0, : t + TILE, kv]) * (d * rows) ** (-0.5)
                 tail = jnp.where(col <= row, a[:, t:], 0.0)
                 a = jnp.concatenate([a[:, :t], tail], axis=1) if t else tail
                 intra = jnp.dot(
                     a.astype(jnp.bfloat16),
-                    v_ref[: t + TILE, kv],
+                    kv_ref[1, : t + TILE, kv],
                     preferred_element_type=jnp.float32,
                 )
                 lane = head * (levels + 1)
@@ -268,19 +277,19 @@
                 side_ref[at, cols] = out
 
 
-def window_kernel(heads, groups, behind, at_ref, q_ref, own_ref, other_ref, *refs):
+def window_kernel(heads, groups, behind, picks, at_ref, q_ref, own_ref, other_ref, *refs):
     d = HEAD_SIZE
     back = refs[:behind]
     side_in, side_ref = refs[behind:]
     rows = q_ref.shape[0]
     here = at_ref[0]
-    pick = at_ref[1] != 0
+    pick = (at_ref[0] & 1) != 0 if picks else True
 
     def run(general):
         def body(g):
             kx, vx = pair(back[-1], g)
             ky, vy = pair(other_ref, g)
-            near = (jnp.where(pick, kx, ky), jnp.where(pick, vx, vy))
+            near = (jnp.where(pick, kx, ky), jnp.where(pick, vx, vy)) if picks else (kx, vx)
             k, v_ext = joined([pair(r, g) for r in back[:-1]] + [near, pair(own_ref, g)])
             for h in range(heads):
                 cols = span(g, heads * d, h * d)
@@ -354,13 +363,16 @@
     full = jax.ShapeDtypeStruct((rows, q_win.shape[1]), f32)
     kv_type = jax.ShapeDtypeStruct((2, rows, k_win.shape[1]), bf16)
 
-    def call(kernel, args, outs, alias=None, scalars=0, work=0.0, limit=24):
+    def call(kernel, args, outs, alias=None, scalars=0, work=0.0, raw=0, copies=0, scratch=(), limit=24):
         keys = work * rows * rows * groups * heads
         return pl.pallas_call(
             kernel,
-            in_specs=[SMEM] * scalars + [VMEM] * (len(args) - scalars),
+            in_specs=[SMEM] * scalars
+            + [pl.BlockSpec(memory_space=pltpu.HBM)] * raw
+            + [VMEM] * (len(args) - scalars - raw),
             out_specs=[VMEM] * len(outs),
             out_shape=outs,
+            scratch_shapes=[*scratch] + [pltpu.SemaphoreType.DMA((copies,))] * (copies > 0),
             input_output_aliases=alias or {},
             compiler_params=pltpu.CompilerParams(vmem_limit_bytes=limit << 20),
             cost_estimate=pl.CostEstimate(
@@ -368,12 +380,29 @@
             ),
         )(*args)
 
+    def on_chip(*blocks):
+        return [pltpu.with_memory_space_constraint(b, pltpu.VMEM) for b in blocks]
+
     part = functools.partial
-    at = jnp.stack([here, here & 1])
-    (shared,) = call(pack_kernel, [k_shared, v_shared], [kv_type])
-    (near,) = call(pack_kernel, [k_win, v_win], [kv_type])
-    state, half = call(
-        state_kernel, [k_lin, v_lin], [jax.ShapeDtypeStruct((groups, d, d), t) for t in (f32, bf16)]
+    at = here.reshape(1)
+    k_shared, v_shared, k_win, v_win, k_lin, v_lin = (
+        pltpu.with_memory_space_constraint(x, pltpu.HBM)
+        for x in (k_shared, v_shared, k_win, v_win, k_lin, v_lin)
+    )
+    (shared,) = call(pack_kernel, [k_shared, v_shared], [kv_type], raw=2, copies=2, limit=4)
+    (near,) = call(pack_kernel, [k_win, v_win], [kv_type], raw=2, copies=2, limit=4)
+    index = level_index.reshape(1, rows)
+    table = level_table.transpose(1, 2, 0)
+    kernel = lambda f, *extra: part(f, heads, groups, *extra)
+    side, weights, state, half = call(
+        kernel(intra_kernel, levels),
+        [k_lin, v_lin, q_lin, index, table],
+        [full, jax.ShapeDtypeStruct((rows, table.shape[0] * table.shape[1]), f32)]
+        + [jax.ShapeDtypeStruct((groups, d, d), t) for t in (f32, bf16)],
+        raw=2,
+        copies=2,
+        scratch=[pltpu.VMEM(kv_type.shape, bf16)],
+        work=0.75,
     )
     buckets = []
     for level in range(levels):
@@ -382,18 +411,9 @@
         state = state + arrived.astype(f32)
         half = state.astype(bf16)
 
-    index = level_index.reshape(rows, 1)
-    table = level_table.reshape(level_table.shape[0], -1)
     gain = jnp.repeat(head_gain, d).reshape(1, -1)
 
-    kernel = lambda f, *extra: part(f, heads, groups, *extra)
     carry = tuple(call(kernel(local_kernel), [q_cross, shared], [full] * 3, work=0.75))
-    side, weights = call(
-        kernel(intra_kernel, levels),
-        [q_lin, k_lin, v_lin, index, table],
-        [full, jax.ShapeDtypeStruct((rows, table.shape[1]), f32)],
-        work=0.75,
-    )
 
     def piece(lives, kvs, carry, where=at):
         n = len(kvs) + 2
@@ -408,10 +428,10 @@
             )
         )
 
-    def windowed(side, back, other, flags):
+    def windowed(side, back, other, picks):
         return call(
-            kernel(window_kernel, behind),
-            [flags, q_win, near, other, *back, side],
+            kernel(window_kernel, behind, picks),
+            [at, q_win, near, other, *back, side],
             [full],
             alias={4 + behind: 0},
             scalars=1,
@@ -444,7 +464,7 @@
             return lambda ref: ref[0] >= 2 * steps
 
         def across(steps):
-            return lambda ref: (ref[0] >= 2 * steps) if steps else (ref[1] == 1)
+            return lambda ref: (ref[0] >= 2 * steps) if steps else ((ref[0] & 1) == 1)
 
         sides = [(2 * i, 2 * i + 1) for i in range(count // 2)]
         z1 = shifted(shared, "ctx", 2)
@@ -457,15 +477,15 @@
         wb = lax.ppermute(w2, "ctx", [(b, a) for a, b in sides])
         x3 = partner(z3, "ctx", 0)
         x2 = partner(z2, "ctx", 0)
-        carry = piece([across(0), straight(1)], [x0, z1], carry)
-        carry = piece([across(1), straight(3)], [x1, z3], carry)
-        side = windowed(side, [w2, wx], wb, at)
-        carry = piece([across(3), straight(2)], [x3, z2], carry)
+        carry = piece([across(0), straight(1)], on_chip(x0, z1), carry)
+        carry = piece([across(1), straight(3)], on_chip(x1, z3), carry)
+        side = windowed(side, on_chip(w2, wx), *on_chip(wb), True)
+        carry = piece([across(3), straight(2)], on_chip(x3, z2), carry)
         side = read(side)
         comb, sq = last(across(2), x2, carry, side)
     else:
         back = [shifted(near, "ctx", step) for step in range(behind, 0, -1)]
-        side = read(windowed(side, back, back[-1], jnp.stack([here, here * 0 + 1])))
+        side = read(windowed(side, back, back[-1], False))
         every = lax.all_gather(shared, "ctx", axis=0, tiled=False)
 
         def step(source, carried):

time: 124 us -> 126 us (1.016)
  the two profiles are of different devices: /device:TPU:25 before, /device:TPU:30 now
where the time goes in v3:
time: 126 us; the launch traced here: 124 us
  Pallas kernels  47.4 us (38%)
  waiting for transfers between devices  35.6 us (28%)
  starting transfers between devices  22.7 us (18%)
  local copies, waits for them, and re-layouts  17.5 us (14%)
    pallas_call x10, Pallas kernels, call(): pl.pallas_call(kernel, in_specs=[SMEM] * scalars + [pl.BlockSpec(memory_s...  45.2 us
    ppermute x7, waiting for transfers between devices, partner(): return lax.ppermute(block, axis, route)  31.9 us
    unnamed x50, local copies, waits for them, and re-layouts  17.4 us
    ppermute x7, starting transfers between devices, partner(): return lax.ppermute(block, axis, route)  8.23 us
    ppermute x1, starting transfers between devices, per_device(): wb = lax.ppermute(w2, 'ctx', [(b, a) for a, b in sides])  6.13 us
    ppermute x4, starting transfers between devices, shifted(): lax.ppermute(value, axis, [(source, source + steps) for source in range(f...  5.14 us
  transfers between devices with their start and end apart: 16, of which 3 were waited for; matrix products, arithmetic and copies ran while one was open for 1% of the time, Pallas kernels for 31%

profile of v3, /device:TPU:30, one launch (start us, length us, event | category | flops | bytes accessed | tf_op | source)
XLA Modules:
  0.0 124.4 jit_solution(7364810432144650720)
XLA Ops:
  0.0 1.9 %shard_map.118.kv_ref = bf16[2,256,512]{2,1,0:T(8,128)(2,1)} custom-call(bf16[256,512]{1,0:T(8,128)(2,1)} %k_ref.3, bf16[256,512]{1,0:T(8,128)(2,1)} %v_ref.3), custom_call_target="tpu_custom_call" | custom-call | flops 1024 | bytes 1048576 | tf_op jit(solution)/shard_map/pallas_call | solution.py:368
  1.9 1.3 %collective-permute-start = (bf16[2,256,512]{2,1,0:T(8,128)(2,1)}, bf16[2,256,512]{2,1,0:T(8,128)(2,1)}, u32[]{:S(2)}, u32[]{:S(2)}) collective-permute-start(bf16[2,256,512]{2,1,0:T(8,128)(2,1)} %shard_map.118.kv_ref), channel_id=1, source_target_pairs={{0,8},{4,12},{8,16},{12,20},{16,24},{20,28},{1,9},{5,13},{9,17},{1... | collective-permute-start | bytes 1572872 | tf_op jit(solution)/shard_map/ppermute | solution.py:25
  3.2 0.0 copy-start.13
  3.2 1.2 copy-done.13
  4.5 0.8 copy-done.22
  5.2 0.7 copy-done.23
  5.9 4.0 %shard_map.123 = (f32[256,2048]{1,0:T(8,128)S(1)}, f32[256,64]{1,0:T(8,128)S(1)}, f32[4,128,128]{2,1,0:T(8,128)S(1)}, bf16[4,128,128]{2,1,0:T(8,128)(2,1)S(1)}) custom-call(bf16[256,512]{1,0:T(8,128)(2,1)} %k_ref.4, bf16[256,512]{1,0:T(8,128)(2,1)} %v_ref.4, bf16[256,2048]{1,0:T(8,128)(2,1)S(1)} %copy-done.13, s32[1,256]{1,0:T(1,128)S(1)} %bitcast.6, ...), custom_call_target="tpu_custom_call" | custom-call | flops 402654208 | bytes 1048576 | tf_op jit(solution)/shard_map/pallas_call | solution.py:368
  9.9 0.6 collective-permute-start.7
  10.5 1.9 %shard_map.124.own_ref = bf16[2,256,512]{2,1,0:T(8,128)(2,1)} custom-call(bf16[256,512]{1,0:T(8,128)(2,1)} %k_ref.5, bf16[256,512]{1,0:T(8,128)(2,1)} %v_ref.5), custom_call_target="tpu_custom_call" | custom-call | flops 1024 | bytes 1048576 | tf_op jit(solution)/shard_map/pallas_call | solution.py:368
  12.4 1.3 %collective-permute-start.10 = (bf16[2,256,512]{2,1,0:T(8,128)(2,1)}, bf16[2,256,512]{2,1,0:T(8,128)(2,1)}, u32[]{:S(2)}, u32[]{:S(2)}) collective-permute-start(bf16[2,256,512]{2,1,0:T(8,128)(2,1)} %shard_map.124.own_ref), channel_id=1, source_target_pairs={{0,8},{4,12},{8,16},{12,20},{16,24},{20,28},{1,9},{5,13},{9,17},{1... | collective-permute-start | bytes 1572872 | tf_op jit(solution)/shard_map/ppermute | solution.py:25
  13.7 1.6 %collective-permute-start.6 = (bf16[2,256,512]{2,1,0:T(8,128)(2,1)}, bf16[2,256,512]{2,1,0:T(8,128)(2,1)S(1)}, u32[]{:S(2)}, u32[]{:S(2)}) collective-permute-start(bf16[2,256,512]{2,1,0:T(8,128)(2,1)} %shard_map.118.kv_ref), channel_id=1, source_target_pairs={{0,4},{4,0},{8,12},{12,8},{16,20},{20,16},{24,28},{28,24},{1,5},{5... | collective-permute-start | bytes 1572872 | tf_op jit(solution)/shard_map/ppermute | solution.py:35
  15.2 1.3 %collective-permute-start.3 = (bf16[2,256,512]{2,1,0:T(8,128)(2,1)}, bf16[2,256,512]{2,1,0:T(8,128)(2,1)}, u32[]{:S(2)}, u32[]{:S(2)}) collective-permute-start(bf16[2,256,512]{2,1,0:T(8,128)(2,1)} %shard_map.118.kv_ref), channel_id=1, source_target_pairs={{0,24},{4,28},{1,25},{5,29},{2,26},{6,30},{3,27},{7,31}} | collective-permute-start | bytes 1572872 | tf_op jit(solution)/shard_map/ppermute | solution.py:25
  16.5 1.8 %collective-permute-done.refs_1_ = bf16[2,256,512]{2,1,0:T(8,128)(2,1)} collective-permute-done((bf16[2,256,512]{2,1,0:T(8,128)(2,1)}, bf16[2,256,512]{2,1,0:T(8,128)(2,1)}, u32[]{:S(2)}, u32[]{:S(2)}) %collective-permute-start) | collective-permute-done | bytes 524320 | tf_op jit(solution)/shard_map/ppermute | solution.py:25
  18.3 1.3 %collective-permute-start.1 = (bf16[2,256,512]{2,1,0:T(8,128)(2,1)}, bf16[2,256,512]{2,1,0:T(8,128)(2,1)}, u32[]{:S(2)}, u32[]{:S(2)}) collective-permute-start(bf16[2,256,512]{2,1,0:T(8,128)(2,1)} %collective-permute-done.refs_1_), channel_id=1, source_target_pairs={{0,8},{4,12},{8,16},{12,20},{16,24},{20,28},{1,9},{5,13},{9,17},{1... | collective-permute-start | bytes 1572872 | tf_op jit(solution)/shard_map/ppermute | solution.py:25
  19.6 0.0 collective-permute-done.7.refs_0_
  19.6 2.7 %collective-permute-start.8 = (bf16[4,128,128]{2,1,0:T(8,128)(2,1)S(1)}, bf16[4,128,128]{2,1,0:T(8,128)(2,1)S(1)}, u32[]{:S(2)}, u32[]{:S(2)}) collective-permute-start(bf16[4,128,128]{2,1,0:T(8,128)(2,1)S(1)} %fusion), channel_id=1, source_target_pairs={{0,8},{8,0},{4,12},{12,4},{16,24},{24,16},{20,28},{28,20},{1,9},{9... | collective-permute-start | bytes 393224 | tf_op jit(solution)/shard_map/ppermute | solution.py:35
  22.3 31.9 %collective-permute-done.8.refs_1_ = bf16[4,128,128]{2,1,0:T(8,128)(2,1)S(1)} collective-permute-done((bf16[4,128,128]{2,1,0:T(8,128)(2,1)S(1)}, bf16[4,128,128]{2,1,0:T(8,128)(2,1)S(1)}, u32[]{:S(2)}, u32[]{:S(2)}) %collective-permute-start.8) | collective-permute-done | bytes 131104 | tf_op jit(solution)/shard_map/ppermute | solution.py:35
  54.2 1.3 %collective-permute-start.12 = (bf16[2,256,512]{2,1,0:T(8,128)(2,1)}, bf16[2,256,512]{2,1,0:T(8,128)(2,1)}, u32[]{:S(2)}, u32[]{:S(2)}) collective-permute-start(bf16[2,256,512]{2,1,0:T(8,128)(2,1)} %shard_map.124.own_ref), channel_id=1, source_target_pairs={{0,4},{8,12},{16,20},{24,28},{1,5},{9,13},{17,21},{25,29},{2,6},{1... | collective-permute-start | bytes 1572872 | tf_op jit(solution)/shard_map/ppermute | solution.py:473
  55.5 0.0 collective-permute-done.10.refs_0_
  55.5 6.1 %collective-permute-start.11 = (bf16[2,256,512]{2,1,0:T(8,128)(2,1)}, bf16[2,256,512]{2,1,0:T(8,128)(2,1)}, u32[]{:S(2)}, u32[]{:S(2)}) collective-permute-start(bf16[2,256,512]{2,1,0:T(8,128)(2,1)} %collective-permute-done.10.refs_0_), channel_id=1, source_target_pairs={{4,0},{12,8},{20,16},{28,24},{5,1},{13,9},{21,17},{29,25},{6,2},{1... | collective-permute-start | bytes 1572872 | tf_op jit(solution)/shard_map/ppermute | solution.py:477
  61.7 0.0 collective-permute-done.6.refs_0_
  61.7 0.0 copy-done.20
  61.7 0.8 copy-done.16
  62.5 0.0 collective-permute-start.5
  62.5 4.4 %shard_map.119 = (f32[256,2048]{1,0:T(8,128)S(1)}, f32[256,2048]{1,0:T(8,128)S(1)}, f32[256,2048]{1,0:T(8,128)S(1)}) custom-call(bf16[256,2048]{1,0:T(8,128)(2,1)S(1)} %copy-done.12, bf16[2,256,512]{2,1,0:T(8,128)(2,1)} %shard_map.118.kv_ref), custom_call_target="tpu_custom_call" | custom-call | flops 402654208 | bytes 1048576 | tf_op jit(solution)/shard_map/pallas_call | solution.py:368
  66.9 0.0 copy-start
  66.9 1.3 %copy-done = f32[256,2048]{1,0:T(8,128)} copy-done((f32[256,2048]{1,0:T(8,128)}, f32[256,2048]{1,0:T(8,128)S(1)}, u32[]{:S(2)}) %copy-start) | copy-done | bytes 2097176
  68.2 1.3 %copy-done.4 = f32[256,2048]{1,0:T(8,128)} copy-done((f32[256,2048]{1,0:T(8,128)}, f32[256,2048]{1,0:T(8,128)S(1)}, u32[]{:S(2)}) %copy-start.4) | copy-done | bytes 2097176
  69.6 1.4 %copy-done.8 = f32[256,2048]{1,0:T(8,128)} copy-done((f32[256,2048]{1,0:T(8,128)}, f32[256,2048]{1,0:T(8,128)S(1)}, u32[]{:S(2)}) %copy-start.8) | copy-done | bytes 2097176
  70.9 0.0 collective-permute-done.3.refs_1_
  70.9 2.0 %collective-permute-start.4 = (bf16[2,256,512]{2,1,0:T(8,128)(2,1)}, bf16[2,256,512]{2,1,0:T(8,128)(2,1)S(1)}, u32[]{:S(2)}, u32[]{:S(2)}) collective-permute-start(bf16[2,256,512]{2,1,0:T(8,128)(2,1)} %collective-permute-done.3.refs_1_), channel_id=1, source_target_pairs={{0,4},{4,0},{8,12},{12,8},{16,20},{20,16},{24,28},{28,24},{1,5},{5... | collective-permute-start | bytes 1572872 | tf_op jit(solution)/shard_map/ppermute | solution.py:35
  73.0 0.0 collective-permute-done.1.refs_1_
  73.0 0.1 collective-permute-start.2
  73.0 1.0 add_convert_fusion
  74.0 0.0 collective-permute-done.12.refs_1_
  74.0 1.3 %collective-permute-start.9 = (bf16[4,128,128]{2,1,0:T(8,128)(2,1)S(1)}, bf16[4,128,128]{2,1,0:T(8,128)(2,1)S(1)}, u32[]{:S(2)}, u32[]{:S(2)}) collective-permute-start(bf16[4,128,128]{2,1,0:T(8,128)(2,1)S(1)} %add_convert_fusion), channel_id=1, source_target_pairs={{0,16},{16,0},{4,20},{20,4},{8,24},{24,8},{12,28},{28,12},{1,17},{... | collective-permute-start | bytes 393224 | tf_op jit(solution)/shard_map/ppermute | solution.py:35
  75.3 1.6 %copy-done.1 = f32[256,2048]{1,0:T(8,128)S(1)} copy-done((f32[256,2048]{1,0:T(8,128)S(1)}, f32[256,2048]{1,0:T(8,128)}, u32[]{:S(2)}) %copy-start.1) | copy-done | bytes 2097176
  76.8 1.6 %copy-done.5 = f32[256,2048]{1,0:T(8,128)S(1)} copy-done((f32[256,2048]{1,0:T(8,128)S(1)}, f32[256,2048]{1,0:T(8,128)}, u32[]{:S(2)}) %copy-start.5) | copy-done | bytes 2097176
  78.4 1.6 %copy-done.9 = f32[256,2048]{1,0:T(8,128)S(1)} copy-done((f32[256,2048]{1,0:T(8,128)S(1)}, f32[256,2048]{1,0:T(8,128)}, u32[]{:S(2)}) %copy-start.9) | copy-done | bytes 2097176
  80.0 1.0 copy-done.17
  81.1 5.8 %shard_map.120 = (f32[256,2048]{1,0:T(8,128)S(1)}, f32[256,2048]{1,0:T(8,128)S(1)}, f32[256,2048]{1,0:T(8,128)S(1)}) custom-call(s32[1]{0:T(128)} %bitcast.at_ref, bf16[256,2048]{1,0:T(8,128)(2,1)S(1)} %copy-done.12, bf16[2,256,512]{2,1,0:T(8,128)(2,1)S(1)} %copy-done.17, ...), custom_call_target="tpu_custom_call", output_to_operand_aliasing={{0}: (4, {}), {1}: (5, {}), {2}: (6, {})} | custom-call | flops 1073742848 | bytes 1048576 | tf_op jit(solution)/shard_map/pallas_call | solution.py:368
  86.9 1.3 %copy-done.2 = f32[256,2048]{1,0:T(8,128)} copy-done((f32[256,2048]{1,0:T(8,128)}, f32[256,2048]{1,0:T(8,128)S(1)}, u32[]{:S(2)}) %copy-start.2) | copy-done | bytes 2097176
  88.2 1.3 %copy-done.6 = f32[256,2048]{1,0:T(8,128)} copy-done((f32[256,2048]{1,0:T(8,128)}, f32[256,2048]{1,0:T(8,128)S(1)}, u32[]{:S(2)}) %copy-start.6) | copy-done | bytes 2097176
  89.6 1.4 %copy-done.10 = f32[256,2048]{1,0:T(8,128)} copy-done((f32[256,2048]{1,0:T(8,128)}, f32[256,2048]{1,0:T(8,128)S(1)}, u32[]{:S(2)}) %copy-start.10) | copy-done | bytes 2097176
  90.9 0.0 collective-permute-done.11.other_ref
  90.9 0.0 copy-done.15
  91.0 8.0 %shard_map.125.refs_3_ = f32[256,2048]{1,0:T(8,128)S(1)} custom-call(s32[1]{0:T(128)} %bitcast.at_ref, bf16[256,2048]{1,0:T(8,128)(2,1)S(1)} %copy-done.15, bf16[2,256,512]{2,1,0:T(8,128)(2,1)} %shard_map.124.own_ref, bf16[2,256,512]{2,1,0:T(8,128)(2,1)} %collective-permute-done.11.other_ref, ...), custom_call_target="tpu_custom_call", output_to_operand_aliasing={{}: (6, {})} | custom-call | flops 1342178304 | bytes 1048576 | tf_op jit(solution)/shard_map/pallas_call | solution.py:368
  98.9 0.0 collective-permute-done.9.refs_2_
  99.0 2.3 %shard_map.126.side_ref = f32[256,2048]{1,0:T(8,128)S(1)} custom-call(s32[1]{0:T(128)} %bitcast.at_ref, bf16[256,2048]{1,0:T(8,128)(2,1)S(1)} %copy-done.14, f32[256,64]{1,0:T(8,128)S(1)} %copy-done.21, bf16[4,128,128]{2,1,0:T(8,128)(2,1)S(1)} %collective-permute-done.7.refs_0_, bf16[4,128,128]{2,1,0:T(8,128)(2,1)S(1)} %copy-done.19, ...), custom_call_target="tpu_custom_call", output_to_operand_aliasing={{}: (6, {})} | custom-call | flops 402654208 | bytes 1048576 | tf_op jit(solution)/shard_map/pallas_call | solution.py:368
  101.3 0.0 collective-permute-done.5.refs_0_
  101.3 6.0 %shard_map.121 = (f32[256,2048]{1,0:T(8,128)S(1)}, f32[256,2048]{1,0:T(8,128)S(1)}, f32[256,2048]{1,0:T(8,128)S(1)}) custom-call(s32[1]{0:T(128)} %bitcast.at_ref, bf16[256,2048]{1,0:T(8,128)(2,1)S(1)} %copy-done.12, bf16[2,256,512]{2,1,0:T(8,128)(2,1)} %collective-permute-done.5.refs_0_, ...), custom_call_target="tpu_custom_call", output_to_operand_aliasing={{0}: (4, {}), {1}: (5, {}), {2}: (6, {})} | custom-call | flops 1073742848 | bytes 1048576 | tf_op jit(solution)/shard_map/pallas_call | solution.py:368
  107.4 0.0 collective-permute-done.4.refs_0_
  107.4 0.0 copy-start.24
  107.4 5.7 %shard_map.122 = (f32[256,2048]{1,0:T(8,128)S(1)}, f32[256,2048]{1,0:T(8,128)S(1)}, f32[256,2048]{1,0:T(8,128)S(1)}) custom-call(s32[1]{0:T(128)} %bitcast.at_ref, bf16[256,2048]{1,0:T(8,128)(2,1)S(1)} %copy-done.12, bf16[2,256,512]{2,1,0:T(8,128)(2,1)S(1)} %collective-permute-done.4.refs_0_, ...), custom_call_target="tpu_custom_call", output_to_operand_aliasing={{0}: (4, {}), {1}: (5, {}), {2}: (6, {})} | custom-call | flops 1073742848 | bytes 1048576 | tf_op jit(solution)/shard_map/pallas_call | solution.py:368
  113.1 0.0 collective-permute-done.2.kv_ref
  113.1 0.1 broadcast_in_dim.3
  113.2 5.3 %shard_map.127 = (f32[256,2048]{1,0:T(8,128)S(1)}, f32[8,256]{1,0:T(8,128)S(1)}) custom-call(s32[1]{0:T(128)} %bitcast.at_ref, bf16[256,2048]{1,0:T(8,128)(2,1)S(1)} %copy-done.12, bf16[2,256,512]{2,1,0:T(8,128)(2,1)S(1)} %collective-permute-done.2.kv_ref, f32[256,2048]{1,0:T(8,128)S(1)} %get-tuple-element.32.acc_in, ...), custom_call_target="tpu_custom_call", output_to_operand_aliasing={{0}: (6, {})} | custom-call | flops 536871936 | bytes 1048576 | tf_op jit(solution)/shard_map/pallas_call | solution.py:368
  118.5 0.0 collective-permute-start.13
  118.5 0.6 collective-permute-start.14
  119.0 1.3 %collective-permute-start.15 = (f32[8,256]{1,0:T(8,128)S(1)}, f32[8,256]{1,0:T(8,128)S(1)}, u32[]{:S(2)}, u32[]{:S(2)}) collective-permute-start(f32[8,256]{1,0:T(8,128)S(1)} %get-tuple-element.40.refs_0_), channel_id=1, source_target_pairs={{0,3},{1,2},{2,1},{3,0},{4,7},{5,6},{6,5},{7,4},{8,11},{9,10},{10,... | collective-permute-start | bytes 24584 | tf_op jit(solution)/shard_map/ppermute | solution.py:502
  120.4 0.0 collective-permute-done.13.refs_1_
  120.4 1.8 %collective-permute-done.14.refs_2_ = f32[8,256]{1,0:T(8,128)S(1)} collective-permute-done((f32[8,256]{1,0:T(8,128)S(1)}, f32[8,256]{1,0:T(8,128)S(1)}, u32[]{:S(2)}, u32[]{:S(2)}) %collective-permute-start.14) | collective-permute-done | bytes 8224 | tf_op jit(solution)/shard_map/ppermute | solution.py:502
  122.2 0.0 collective-permute-done.15.refs_3_
  122.2 2.2 %norm.1 = bf16[256,2048]{1,0:T(8,128)(2,1)} custom-call(f32[256,2048]{1,0:T(8,128)S(1)} %get-tuple-element.39.comb_ref, f32[8,256]{1,0:T(8,128)S(1)} %get-tuple-element.40.refs_0_, f32[8,256]{1,0:T(8,128)S(1)} %collective-permute-done.13.refs_1_, f32[8,256]{1,0:T(8,128)S(1)} %collective-permute-done.14.refs_2_, f32[8,256]{1,0:T(8,128)S(1)} %collective-permute-done.15.refs_3_), custom_call_target="tpu_custom_call" | custom-call | tf_op jit(solution)/shard_map/norm/pallas_call | solution.py:507
  (32 shorter events, 0.1 us)
Async XLA Ops:
  0.0 62.5 %copy-start.12 = (bf16[256,2048]{1,0:T(8,128)(2,1)S(1)}, bf16[256,2048]{1,0:T(8,128)(2,1)}, u32[]{:S(2)}) copy-start(bf16[256,2048]{1,0:T(8,128)(2,1)} %q_ref.15) | copy-start | bytes 3145732
  1.9 16.3 %collective-permute-start = (bf16[2,256,512]{2,1,0:T(8,128)(2,1)}, bf16[2,256,512]{2,1,0:T(8,128)(2,1)}, u32[]{:S(2)}, u32[]{:S(2)}) collective-permute-start(bf16[2,256,512]{2,1,0:T(8,128)(2,1)} %shard_map.118.kv_ref), channel_id=1, source_target_pairs={{0,8},{4,12},{8,16},{12,20},{16,24},{20,28},{1,9},{5,13},{9,17},{1... | collective-permute-start | bytes 1572872 | tf_op jit(solution)/shard_map/ppermute | solution.py:25
  3.2 1.2 copy-start.13
  4.5 0.8 copy-start.22
  5.2 0.7 copy-start.23
  9.9 51.8 %copy-start.20 = (f32[256,64]{1,0:T(8,128)}, f32[256,64]{1,0:T(8,128)S(1)}, u32[]{:S(2)}) copy-start(f32[256,64]{1,0:T(8,128)S(1)} %get-tuple-element.35.w_ref) | copy-start | bytes 196612
  9.9 9.7 %collective-permute-start.7 = (bf16[4,128,128]{2,1,0:T(8,128)(2,1)S(1)}, bf16[4,128,128]{2,1,0:T(8,128)(2,1)S(1)}, u32[]{:S(2)}, u32[]{:S(2)}) collective-permute-start(bf16[4,128,128]{2,1,0:T(8,128)(2,1)S(1)} %get-tuple-element.36), channel_id=1, source_target_pairs={{0,4},{4,0},{8,12},{12,8},{16,20},{20,16},{24,28},{28,24},{1,5},{5... | collective-permute-start | bytes 393224 | tf_op jit(solution)/shard_map/ppermute | solution.py:35
  12.4 43.2 %collective-permute-start.10 = (bf16[2,256,512]{2,1,0:T(8,128)(2,1)}, bf16[2,256,512]{2,1,0:T(8,128)(2,1)}, u32[]{:S(2)}, u32[]{:S(2)}) collective-permute-start(bf16[2,256,512]{2,1,0:T(8,128)(2,1)} %shard_map.124.own_ref), channel_id=1, source_target_pairs={{0,8},{4,12},{8,16},{12,20},{16,24},{20,28},{1,9},{5,13},{9,17},{1... | collective-permute-start | bytes 1572872 | tf_op jit(solution)/shard_map/ppermute | solution.py:25
  13.7 48.0 %collective-permute-start.6 = (bf16[2,256,512]{2,1,0:T(8,128)(2,1)}, bf16[2,256,512]{2,1,0:T(8,128)(2,1)S(1)}, u32[]{:S(2)}, u32[]{:S(2)}) collective-permute-start(bf16[2,256,512]{2,1,0:T(8,128)(2,1)} %shard_map.118.kv_ref), channel_id=1, source_target_pairs={{0,4},{4,0},{8,12},{12,8},{16,20},{20,16},{24,28},{28,24},{1,5},{5... | collective-permute-start | bytes 1572872 | tf_op jit(solution)/shard_map/ppermute | solution.py:35
  15.2 55.7 %collective-permute-start.3 = (bf16[2,256,512]{2,1,0:T(8,128)(2,1)}, bf16[2,256,512]{2,1,0:T(8,128)(2,1)}, u32[]{:S(2)}, u32[]{:S(2)}) collective-permute-start(bf16[2,256,512]{2,1,0:T(8,128)(2,1)} %shard_map.118.kv_ref), channel_id=1, source_target_pairs={{0,24},{4,28},{1,25},{5,29},{2,26},{6,30},{3,27},{7,31}} | collective-permute-start | bytes 1572872 | tf_op jit(solution)/shard_map/ppermute | solution.py:25
  18.3 54.7 %collective-permute-start.1 = (bf16[2,256,512]{2,1,0:T(8,128)(2,1)}, bf16[2,256,512]{2,1,0:T(8,128)(2,1)}, u32[]{:S(2)}, u32[]{:S(2)}) collective-permute-start(bf16[2,256,512]{2,1,0:T(8,128)(2,1)} %collective-permute-done.refs_1_), channel_id=1, source_target_pairs={{0,8},{4,12},{8,16},{12,20},{16,24},{20,28},{1,9},{5,13},{9,17},{1... | collective-permute-start | bytes 1572872 | tf_op jit(solution)/shard_map/ppermute | solution.py:25
  19.6 34.6 %collective-permute-start.8 = (bf16[4,128,128]{2,1,0:T(8,128)(2,1)S(1)}, bf16[4,128,128]{2,1,0:T(8,128)(2,1)S(1)}, u32[]{:S(2)}, u32[]{:S(2)}) collective-permute-start(bf16[4,128,128]{2,1,0:T(8,128)(2,1)S(1)} %fusion), channel_id=1, source_target_pairs={{0,8},{8,0},{4,12},{12,4},{16,24},{24,16},{20,28},{28,20},{1,9},{9... | collective-permute-start | bytes 393224 | tf_op jit(solution)/shard_map/ppermute | solution.py:35
  54.2 7.4 %copy-start.18 = (bf16[4,128,128]{2,1,0:T(8,128)(2,1)}, bf16[4,128,128]{2,1,0:T(8,128)(2,1)S(1)}, u32[]{:S(2)}) copy-start(bf16[4,128,128]{2,1,0:T(8,128)(2,1)S(1)} %collective-permute-done.8.refs_1_) | copy-start | bytes 393220
  54.2 19.8 %collective-permute-start.12 = (bf16[2,256,512]{2,1,0:T(8,128)(2,1)}, bf16[2,256,512]{2,1,0:T(8,128)(2,1)}, u32[]{:S(2)}, u32[]{:S(2)}) collective-permute-start(bf16[2,256,512]{2,1,0:T(8,128)(2,1)} %shard_map.124.own_ref), channel_id=1, source_target_pairs={{0,4},{8,12},{16,20},{24,28},{1,5},{9,13},{17,21},{25,29},{2,6},{1... | collective-permute-start | bytes 1572872 | tf_op jit(solution)/shard_map/ppermute | solution.py:473
  55.5 35.4 %collective-permute-start.11 = (bf16[2,256,512]{2,1,0:T(8,128)(2,1)}, bf16[2,256,512]{2,1,0:T(8,128)(2,1)}, u32[]{:S(2)}, u32[]{:S(2)}) collective-permute-start(bf16[2,256,512]{2,1,0:T(8,128)(2,1)} %collective-permute-done.10.refs_0_), channel_id=1, source_target_pairs={{4,0},{12,8},{20,16},{28,24},{5,1},{13,9},{21,17},{29,25},{6,2},{1... | collective-permute-start | bytes 1572872 | tf_op jit(solution)/shard_map/ppermute | solution.py:477
  61.7 0.8 copy-start.16
  62.5 38.8 %collective-permute-start.5 = (bf16[2,256,512]{2,1,0:T(8,128)(2,1)}, bf16[2,256,512]{2,1,0:T(8,128)(2,1)}, u32[]{:S(2)}, u32[]{:S(2)}) collective-permute-start(bf16[2,256,512]{2,1,0:T(8,128)(2,1)} %collective-permute-done.refs_1_), channel_id=1, source_target_pairs={{0,4},{4,0},{8,12},{12,8},{16,20},{20,16},{24,28},{28,24},{1,5},{5... | collective-permute-start | bytes 1572872 | tf_op jit(solution)/shard_map/ppermute | solution.py:35
  66.9 1.4 %copy-start = (f32[256,2048]{1,0:T(8,128)}, f32[256,2048]{1,0:T(8,128)S(1)}, u32[]{:S(2)}) copy-start(f32[256,2048]{1,0:T(8,128)S(1)} %get-tuple-element.23.refs_2_) | copy-start | bytes 6291460
  68.2 1.3 %copy-start.4 = (f32[256,2048]{1,0:T(8,128)}, f32[256,2048]{1,0:T(8,128)S(1)}, u32[]{:S(2)}) copy-start(f32[256,2048]{1,0:T(8,128)S(1)} %get-tuple-element.24.refs_3_) | copy-start | bytes 6291460
  69.5 1.4 %copy-start.8 = (f32[256,2048]{1,0:T(8,128)}, f32[256,2048]{1,0:T(8,128)S(1)}, u32[]{:S(2)}) copy-start(f32[256,2048]{1,0:T(8,128)S(1)} %get-tuple-element.25.refs_4_) | copy-start | bytes 6291460
  70.9 36.4 %collective-permute-start.4 = (bf16[2,256,512]{2,1,0:T(8,128)(2,1)}, bf16[2,256,512]{2,1,0:T(8,128)(2,1)S(1)}, u32[]{:S(2)}, u32[]{:S(2)}) collective-permute-start(bf16[2,256,512]{2,1,0:T(8,128)(2,1)} %collective-permute-done.3.refs_1_), channel_id=1, source_target_pairs={{0,4},{4,0},{8,12},{12,8},{16,20},{20,16},{24,28},{28,24},{1,5},{5... | collective-permute-start | bytes 1572872 | tf_op jit(solution)/shard_map/ppermute | solution.py:35
  73.0 40.2 %collective-permute-start.2 = (bf16[2,256,512]{2,1,0:T(8,128)(2,1)}, bf16[2,256,512]{2,1,0:T(8,128)(2,1)S(1)}, u32[]{:S(2)}, u32[]{:S(2)}) collective-permute-start(bf16[2,256,512]{2,1,0:T(8,128)(2,1)} %collective-permute-done.1.refs_1_), channel_id=1, source_target_pairs={{0,4},{4,0},{8,12},{12,8},{16,20},{20,16},{24,28},{28,24},{1,5},{5... | collective-permute-start | bytes 1572872 | tf_op jit(solution)/shard_map/ppermute | solution.py:35
  74.0 24.9 %collective-permute-start.9 = (bf16[4,128,128]{2,1,0:T(8,128)(2,1)S(1)}, bf16[4,128,128]{2,1,0:T(8,128)(2,1)S(1)}, u32[]{:S(2)}, u32[]{:S(2)}) collective-permute-start(bf16[4,128,128]{2,1,0:T(8,128)(2,1)S(1)} %add_convert_fusion), channel_id=1, source_target_pairs={{0,16},{16,0},{4,20},{20,4},{8,24},{24,8},{12,28},{28,12},{1,17},{... | collective-permute-start | bytes 393224 | tf_op jit(solution)/shard_map/ppermute | solution.py:35
  75.3 1.6 %copy-start.1 = (f32[256,2048]{1,0:T(8,128)S(1)}, f32[256,2048]{1,0:T(8,128)}, u32[]{:S(2)}) copy-start(f32[256,2048]{1,0:T(8,128)} %copy-done) | copy-start | bytes 6291460
  76.8 1.6 %copy-start.5 = (f32[256,2048]{1,0:T(8,128)S(1)}, f32[256,2048]{1,0:T(8,128)}, u32[]{:S(2)}) copy-start(f32[256,2048]{1,0:T(8,128)} %copy-done.4) | copy-start | bytes 6291460
  78.4 1.6 %copy-start.9 = (f32[256,2048]{1,0:T(8,128)S(1)}, f32[256,2048]{1,0:T(8,128)}, u32[]{:S(2)}) copy-start(f32[256,2048]{1,0:T(8,128)} %copy-done.8) | copy-start | bytes 6291460
  80.0 1.0 copy-start.17
  81.1 9.9 %copy-start.15 = (bf16[256,2048]{1,0:T(8,128)(2,1)S(1)}, bf16[256,2048]{1,0:T(8,128)(2,1)}, u32[]{:S(2)}) copy-start(bf16[256,2048]{1,0:T(8,128)(2,1)} %q_ref.13) | copy-start | bytes 3145732
  86.9 1.3 %copy-start.2 = (f32[256,2048]{1,0:T(8,128)}, f32[256,2048]{1,0:T(8,128)S(1)}, u32[]{:S(2)}) copy-start(f32[256,2048]{1,0:T(8,128)S(1)} %get-tuple-element.26.refs_2_) | copy-start | bytes 6291460
  88.2 1.3 %copy-start.6 = (f32[256,2048]{1,0:T(8,128)}, f32[256,2048]{1,0:T(8,128)S(1)}, u32[]{:S(2)}) copy-start(f32[256,2048]{1,0:T(8,128)S(1)} %get-tuple-element.27.refs_3_) | copy-start | bytes 6291460
  89.6 1.4 %copy-start.10 = (f32[256,2048]{1,0:T(8,128)}, f32[256,2048]{1,0:T(8,128)S(1)}, u32[]{:S(2)}) copy-start(f32[256,2048]{1,0:T(8,128)S(1)} %get-tuple-element.28.refs_4_) | copy-start | bytes 6291460
  90.9 8.0 %copy-start.14 = (bf16[256,2048]{1,0:T(8,128)(2,1)S(1)}, bf16[256,2048]{1,0:T(8,128)(2,1)}, u32[]{:S(2)}) copy-start(bf16[256,2048]{1,0:T(8,128)(2,1)} %q_ref.14) | copy-start | bytes 3145732
  90.9 8.0 %copy-start.19 = (bf16[4,128,128]{2,1,0:T(8,128)(2,1)S(1)}, bf16[4,128,128]{2,1,0:T(8,128)(2,1)}, u32[]{:S(2)}) copy-start(bf16[4,128,128]{2,1,0:T(8,128)(2,1)} %copy-done.18) | copy-start | bytes 393220
  90.9 8.0 %copy-start.21 = (f32[256,64]{1,0:T(8,128)S(1)}, f32[256,64]{1,0:T(8,128)}, u32[]{:S(2)}) copy-start(f32[256,64]{1,0:T(8,128)} %copy-done.20) | copy-start | bytes 196612
  91.0 10.3 %copy-start.11 = (f32[256,2048]{1,0:T(8,128)S(1)}, f32[256,2048]{1,0:T(8,128)}, u32[]{:S(2)}) copy-start(f32[256,2048]{1,0:T(8,128)} %copy-done.10) | copy-start | bytes 6291460
  99.0 2.3 %copy-start.3 = (f32[256,2048]{1,0:T(8,128)S(1)}, f32[256,2048]{1,0:T(8,128)}, u32[]{:S(2)}) copy-start(f32[256,2048]{1,0:T(8,128)} %copy-done.2) | copy-start | bytes 6291460
  99.0 2.3 %copy-start.7 = (f32[256,2048]{1,0:T(8,128)S(1)}, f32[256,2048]{1,0:T(8,128)}, u32[]{:S(2)}) copy-start(f32[256,2048]{1,0:T(8,128)} %copy-done.6) | copy-start | bytes 6291460
  107.4 5.7 %copy-start.24 = (f32[16]{0:T(128)S(1)}, f32[16]{0:T(128)}, u32[]{:S(2)}) copy-start(f32[16]{0:T(128)} %param.23) | copy-start | bytes 196
  118.5 1.9 %collective-permute-start.13 = (f32[8,256]{1,0:T(8,128)S(1)}, f32[8,256]{1,0:T(8,128)S(1)}, u32[]{:S(2)}, u32[]{:S(2)}) collective-permute-start(f32[8,256]{1,0:T(8,128)S(1)} %get-tuple-element.40.refs_0_), channel_id=1, source_target_pairs={{0,1},{1,0},{2,3},{3,2},{4,5},{5,4},{6,7},{7,6},{8,9},{9,8},{10,11... | collective-permute-start | bytes 24584 | tf_op jit(solution)/shard_map/ppermute | solution.py:502
  118.5 3.7 %collective-permute-start.14 = (f32[8,256]{1,0:T(8,128)S(1)}, f32[8,256]{1,0:T(8,128)S(1)}, u32[]{:S(2)}, u32[]{:S(2)}) collective-permute-start(f32[8,256]{1,0:T(8,128)S(1)} %get-tuple-element.40.refs_0_), channel_id=1, source_target_pairs={{0,2},{1,3},{2,0},{3,1},{4,6},{5,7},{6,4},{7,5},{8,10},{9,11},{10,... | collective-permute-start | bytes 24584 | tf_op jit(solution)/shard_map/ppermute | solution.py:502
  119.0 3.2 %collective-permute-start.15 = (f32[8,256]{1,0:T(8,128)S(1)}, f32[8,256]{1,0:T(8,128)S(1)}, u32[]{:S(2)}, u32[]{:S(2)}) collective-permute-start(f32[8,256]{1,0:T(8,128)S(1)} %get-tuple-element.40.refs_0_), channel_id=1, source_target_pairs={{0,3},{1,2},{2,1},{3,0},{4,7},{5,6},{6,5},{7,4},{8,11},{9,10},{10,... | collective-permute-start | bytes 24584 | tf_op jit(solution)/shard_map/ppermute | solution.py:502
